TPU v7x, 32 devices: a whole 2x2x4 slice. The times are simulated.
32 devices in a mesh: patch: 16 (over z, y, x), grp: 2 (over core).
Axes of the slice: x: 2, y: 2, z: 4, core: 2. Of those that a mesh axis runs over, the one named last changes fastest.
Arguments:
- node_latent: float32 [5120, 512], P(('patch', 'grp')), may hold values from -6 to 6
- edge_latent: float32 [32768, 512], P(('patch', 'grp')), may hold values from -6 to 6
- node_cot: float32 [5120, 512], P(('patch', 'grp')), may hold values from -6 to 6
- edge_cot: float32 [32768, 512], P(('patch', 'grp')), may hold values from -6 to 6
- edge_w1: bfloat16 [1536, 512], replicated, may hold values from -0.15625 to 0.15625
- edge_w2: bfloat16 [512, 512], replicated, may hold values from -0.25 to 0.25
- edge_gain: float32 [512], replicated, may hold values from 0.1 to 1.9
- node_w1: bfloat16 [1024, 512], replicated, may hold values from -0.1875 to 0.1875
- node_w2: bfloat16 [512, 512], replicated, may hold values from -0.25 to 0.25
- node_gain: float32 [512], replicated, may hold values from 0.1 to 1.9
- senders: int32 [32768], P(('patch', 'grp')), may hold values from 0 to 959, as said below
- receivers: int32 [32768], P(('patch', 'grp')), may hold values from 0 to 319
- counts: int32 [32], P(('patch', 'grp')), may hold values from 256 to 1024, as said below
Outputs:
- node_grad: float32 [5120, 512], P(('patch', 'grp'))
- edge_grad: float32 [32768, 512], P(('patch', 'grp'))
- grad_edge_w1: float32 [1536, 512], P('grp')
- grad_edge_w2: float32 [512, 512], P('grp')
- grad_node_w1: float32 [1024, 512], P('grp')
- grad_node_w2: float32 [512, 512], P('grp')
Inputs may be any that keep to these rules, and one draw needn't show every extreme that they name: `senders`: indices into the nodes of the previous patch, the own patch and the next patch (patches taken cyclically), 320 rows each, in that order. `counts`: each device's live edges fill its first slots; some device is full in every draw.
All inputs are finite; a program needn't handle non-finite values.
Results may differ from a plain program's by a relative error of at most 0.0068.
Values may be sent and summed in bfloat16 or wider, within the bound.
A program may use at most 128 MiB of HBM per device.

v0:
```python
import jax
import jax.numpy as jnp
from jax import lax
from jax.sharding import PartitionSpec as P

EPS = 1e-05


def extended_2(x, sides, width):
    for axis, dim in sides:
        peers, length = (lax.axis_size(axis), x.shape[dim])
        up = [(i, (i + 1) % peers) for i in range(peers)]
        down = [(j, i) for i, j in up]
        last = lax.slice_in_dim(x, length - width, length, axis=dim)
        first = lax.slice_in_dim(x, 0, width, axis=dim)
        before = lax.ppermute(last, axis, up)
        after = lax.ppermute(first, axis, down)
        x = jnp.concatenate([before, x, after], axis=dim)
    return x


def shifted(value, axis, steps):
    count = lax.axis_size(axis)
    pairs = [(source, (source + steps) % count) for source in range(count)]
    return lax.ppermute(value, axis, pairs)


def silu_grad(pre):
    sig = jax.nn.sigmoid(pre)
    return sig * (1.0 + pre * (1.0 - sig))


def norm_forward(out, gain):
    center = out - jnp.mean(out, axis=-1, keepdims=True)
    inv_std = lax.rsqrt(jnp.mean(center * center, axis=-1, keepdims=True) + EPS)
    normed = center * inv_std
    return (normed * gain, normed, inv_std)


def norm_backward(grad_y, gain, normed, inv_std):
    scaled = grad_y * gain
    return inv_std * (
        scaled
        - jnp.mean(scaled, axis=-1, keepdims=True)
        - normed * jnp.mean(scaled * normed, axis=-1, keepdims=True)
    )


def mlp_forward(inputs, first, second, gain):
    pre = jnp.dot(inputs, first, preferred_element_type=jnp.float32)
    act = jax.nn.silu(pre).astype(jnp.bfloat16)
    out = jnp.dot(act, second, preferred_element_type=jnp.float32)
    upd, normed, inv_std = norm_forward(out, gain)
    return (upd, pre, act, normed, inv_std)


def mlp_backward(grad_y, inputs, first, second, gain, pre, act, normed, inv_std):
    grad_out = norm_backward(grad_y, gain, normed, inv_std).astype(jnp.bfloat16)
    grad_second = jnp.dot(act.T, grad_out, preferred_element_type=jnp.float32)
    grad_act = jnp.dot(grad_out, second.T, preferred_element_type=jnp.float32)
    grad_pre = (grad_act * silu_grad(pre)).astype(jnp.bfloat16)
    grad_first = jnp.dot(inputs.T, grad_pre, preferred_element_type=jnp.float32)
    grad_in = jnp.dot(grad_pre, first.T, preferred_element_type=jnp.float32)
    return (grad_in, grad_first, grad_second)


def local(
    node_latent,
    edge_latent,
    node_cot,
    edge_cot,
    edge_w1,
    edge_w2,
    edge_gain,
    node_w1,
    node_w2,
    node_gain,
    senders,
    receivers,
    counts,
):
    width = node_latent.shape[1]
    patch_rows = node_latent.shape[0] * lax.axis_size("grp")
    node_bf = node_latent.astype(jnp.bfloat16)
    patch_nodes = lax.all_gather(node_bf, "grp", axis=0, tiled=True)
    extended = extended_2(patch_nodes, (("patch", 0),), patch_rows)
    slot_ids = jnp.arange(edge_latent.shape[0], dtype=jnp.int32)
    live = (slot_ids < counts[0]).astype(jnp.float32)[:, None]
    edge_in = jnp.concatenate(
        [edge_latent.astype(jnp.bfloat16), extended[senders], patch_nodes[receivers]], axis=1
    )
    edge_upd, edge_pre, edge_act, edge_normed, edge_inv = mlp_forward(
        edge_in, edge_w1, edge_w2, edge_gain
    )
    edge_upd = edge_upd * live
    partial_agg = jax.ops.segment_sum(edge_upd, receivers, num_segments=patch_rows)
    aggregate = lax.psum_scatter(partial_agg, "grp", scatter_dimension=0, tiled=True)
    node_in = jnp.concatenate([node_bf, aggregate.astype(jnp.bfloat16)], axis=1)
    node_upd, node_pre, node_act, node_normed, node_inv = mlp_forward(
        node_in, node_w1, node_w2, node_gain
    )
    node_gin, grad_node_w1, grad_node_w2 = mlp_backward(
        node_cot, node_in, node_w1, node_w2, node_gain, node_pre, node_act, node_normed, node_inv
    )
    grad_patch = lax.all_gather(node_gin[:, width:], "grp", axis=0, tiled=True)
    edge_gupd = (edge_cot + grad_patch[receivers]) * live
    edge_gin, grad_edge_w1, grad_edge_w2 = mlp_backward(
        edge_gupd, edge_in, edge_w1, edge_w2, edge_gain, edge_pre, edge_act, edge_normed, edge_inv
    )
    edge_grad = edge_cot + edge_gin[:, :width]
    sent = jax.ops.segment_sum(edge_gin[:, width : 2 * width], senders, num_segments=3 * patch_rows)
    recvd = jax.ops.segment_sum(edge_gin[:, 2 * width :], receivers, num_segments=patch_rows)
    before = sent[:patch_rows]
    middle = sent[patch_rows : 2 * patch_rows] + recvd
    after = sent[2 * patch_rows :]
    from_next = shifted(before, "patch", -1)
    from_prev = shifted(after, "patch", 1)
    share = lax.psum_scatter(middle + from_next + from_prev, "grp", scatter_dimension=0, tiled=True)
    node_grad = node_cot + node_gin[:, :width] + share
    pieces_w = (
        lax.psum_scatter(grad_edge_w1, "grp", scatter_dimension=0, tiled=True),
        lax.psum_scatter(grad_edge_w2, "grp", scatter_dimension=0, tiled=True),
        lax.psum_scatter(grad_node_w1, "grp", scatter_dimension=0, tiled=True),
        lax.psum_scatter(grad_node_w2, "grp", scatter_dimension=0, tiled=True),
    )
    results = lax.psum((pieces_w[0], pieces_w[1], pieces_w[2], pieces_w[3]), "patch")
    return (node_grad, edge_grad, results[0], results[1], results[2], results[3])


def solution(mesh):
    in_specs = (
        P(("patch", "grp"), None),
        P(("patch", "grp"), None),
        P(("patch", "grp"), None),
        P(("patch", "grp"), None),
        P(),
        P(),
        P(),
        P(),
        P(),
        P(),
        P(("patch", "grp")),
        P(("patch", "grp")),
        P(("patch", "grp")),
    )
    out_specs = (
        P(("patch", "grp"), None),
        P(("patch", "grp"), None),
        P("grp", None),
        P("grp", None),
        P("grp", None),
        P("grp", None),
    )
    return jax.shard_map(local, mesh=mesh, in_specs=in_specs, out_specs=out_specs, check_vma=False)
```

profile of v0, /device:TPU:0, one launch (start us, length us, event | category | flops | bytes accessed | tf_op | source)
XLA Modules:
  0.0 339.9 jit_solution(5344323767794569617)
XLA Ops:
  8.3 2.2 all_gather.6
  10.5 2.8 collective-permute-start
  13.3 4.0 %collective-permute-start.1 = (bf16[320,512]{1,0:T(8,128)(2,1)S(1)}, bf16[320,512]{1,0:T(8,128)(2,1)}, u32[]{:S(2)}, u32[]{:S(2)}) collective-permute-start(bf16[320,512]{1,0:T(8,128)(2,1)S(1)} %all_gather.6), channel_id=1, source_target_pairs={{2,0},{4,2},{6,4},{8,6},{10,8},{12,10},{14,12},{16,14},{18,16},{20... | collective-permute-start | bytes 983048 | tf_op jit(solution)/shard_map/ppermute | solution.py:17
  18.0 5.1 %gather_fusion.1 = bf16[1024,512]{1,0:T(8,128)(2,1)} fusion(bf16[320,512]{1,0:T(8,128)(2,1)S(1)} %all_gather.6, s32[1024]{0:T(1024)S(1)} %fusion.15), kind=kCustom, calls=%fused_computation.1 | custom fusion | bytes 2101248 | tf_op jit(solution)/shard_map/gather | solution.py:90
  23.1 2.8 convert_element_type.35
  27.6 2.1 collective-permute-done.1
  30.7 5.1 %gather_fusion = bf16[1024,512]{1,0:T(8,128)(2,1)} fusion(bf16[960,512]{1,0:T(8,128)(2,1)S(1)} %pad_maximum_fusion.3, s32[1024]{0:T(1024)S(1)} %fusion.14), kind=kCustom, calls=%fused_computation | custom fusion | bytes 2101248 | tf_op jit(solution)/shard_map/gather | solution.py:90
  35.8 5.2 %multiply_convert_fusion.2 = (bf16[1024,512]{1,0:T(8,128)(2,1)S(1)}, f32[1024,512]{1,0:T(8,128)}) fusion(bf16[1536,512]{1,0:T(8,128)(2,1)S(1)} %copy-done, bf16[1024,512]{1,0:T(8,128)(2,1)} %gather_fusion.1, bf16[1024,512]{1,0:T(8,128)(2,1)} %gather_fusion, bf16[1024,512]{1,0:T(8,128)(2,1)} %convert_element_type.35), kind=kOutput, calls=%fused_computation.18 | convolution fusion | flops 1622671360 | bytes 7864320 | tf_op jit(solution)/shard_map/dot_general | solution.py:50
  43.2 1.6 multiply_multiply_fusion.1
  44.8 2.9 copy.21
  47.7 8.1 %scatter_custom_fusion = f32[320,512]{1,0:T(8,128)} fusion(s32[1024]{0:T(1024)} %param.24, f32[1024,512]{1,0:T(8,128)} %copy.21, f32[]{:T(128)} %constant.10.clone.1), kind=kCustom, calls=%fused_computation.37 | custom fusion | flops 524288 | bytes 655872 | tf_op jit(solution)/shard_map/scatter-add | solution.py:96
  55.9 3.0 copy.22
  58.8 5.5 %reduce-scatter.7.cloned.1.call-done = f32[160,512]{1,0:T(8,128)} async-done(((f32[320,512]{1,0:T(8,128)}), f32[160,512]{1,0:T(8,128)}) %reduce-scatter.7.cloned.1.call-update) | async-done | bytes 327696 | tf_op jit(solution)/shard_map/reduce_scatter | solution.py:97
  71.0 2.5 all_gather.7
  73.5 4.9 %gather_fusion.2 = f32[1024,512]{1,0:T(8,128)} fusion(f32[320,512]{1,0:T(8,128)S(1)} %all_gather.7, s32[1024]{0:T(1024)S(1)} %fusion.15), kind=kCustom, calls=%fused_computation.2 | custom fusion | bytes 4198400 | tf_op jit(solution)/shard_map/gather | solution.py:106
  78.4 2.9 copy.23
  81.3 3.6 %fusion.23 = (f32[1024]{0:T(1024)S(1)}, f32[1024]{0:T(1024)S(1)}, f32[1024,512]{0,1:T(8,128)S(1)}) fusion(f32[1024]{0:T(1024)S(1)} %add_rsqrt_fusion, f32[1024,512]{0,1:T(8,128)} %copy-done.1, f32[1024]{0:T(1024)S(1)} %broadcast_multiply_fusion.2, f32[512]{0:T(512)S(1)} %copy-done.20, f32[1024]{0:T(1024)S(1)} %fusion.16, f32[1024,512]{0,1:T(8,128)} %copy.22, ...), kind=kLoop, calls=%fused_computation.62 | loop fusion | flops 4192256 | bytes 8411136 | tf_op jit(solution)/shard_map/reduce_sum | solution.py:44
  86.2 1.7 fusion.29
  88.0 1.8 fusion.12
  90.8 3.0 multiply_convert_fusion
  94.8 3.6 %fusion.4 = f32[1536,512]{1,0:T(8,128)} fusion(bf16[1024,512]{1,0:T(8,128)(2,1)S(1)} %multiply_convert_fusion, bf16[1024,512]{1,0:T(8,128)(2,1)S(1)} %copy-done.8, bf16[1024,512]{1,0:T(8,128)(2,1)S(1)} %copy-done.10, bf16[1024,512]{1,0:T(8,128)(2,1)S(1)} %copy-done.9), kind=kOutput, calls=%fused_computation.21 | convolution fusion | flops 1620049920 | bytes 7340032 | tf_op jit(solution)/shard_map/dot_general | solution.py:62
  99.6 4.5 %fusion.28 = f32[1024,1536]{1,0:T(8,128)} fusion(bf16[1024,512]{1,0:T(8,128)(2,1)S(1)} %copy-done.24, bf16[1536,512]{1,0:T(8,128)(2,1)S(1)} %copy-done), kind=kOutput, calls=%fused_computation.67 | convolution fusion | flops 1610612736 | bytes 8912896 | tf_op jit(solution)/shard_map/dot_general | solution.py:63
  104.0 7.9 %scatter_custom_fusion.1 = f32[960,512]{1,0:T(8,128)S(1)} fusion(s32[1024]{0:T(1024)S(1)} %copy-done.21, f32[1024,1536]{1,0:T(8,128)} %fusion.28, f32[]{:T(128)} %constant.10.clone.1), kind=kCustom, calls=%fused_computation.10 | custom fusion | flops 524288 | bytes 4063744 | tf_op jit(solution)/shard_map/scatter-add | solution.py:111
  112.0 5.4 %collective-permute-start.2 = (f32[320,512]{1,0:T(8,128)S(1)}, f32[320,512]{1,0:T(8,128)S(1)}, u32[]{:S(2)}, u32[]{:S(2)}) collective-permute-start(f32[320,512]{1,0:T(8,128)S(1)} %get-tuple-element.15), channel_id=1, source_target_pairs={{0,30},{2,0},{4,2},{6,4},{8,6},{10,8},{12,10},{14,12},{16,14},{18,... | collective-permute-start | bytes 1966088 | tf_op jit(solution)/shard_map/ppermute | solution.py:25
  117.4 14.5 %collective-permute-done.2 = f32[320,512]{1,0:T(8,128)S(1)} collective-permute-done((f32[320,512]{1,0:T(8,128)S(1)}, f32[320,512]{1,0:T(8,128)S(1)}, u32[]{:S(2)}, u32[]{:S(2)}) %collective-permute-start.2) | collective-permute-done | bytes 655392 | tf_op jit(solution)/shard_map/ppermute | solution.py:25
  131.9 12.2 %collective-permute-done.3 = f32[320,512]{1,0:T(8,128)S(1)} collective-permute-done((f32[320,512]{1,0:T(8,128)S(1)}, f32[320,512]{1,0:T(8,128)S(1)}, u32[]{:S(2)}, u32[]{:S(2)}) %collective-permute-start.3) | collective-permute-done | bytes 655392 | tf_op jit(solution)/shard_map/ppermute | solution.py:25
  145.1 9.3 %scatter_custom_fusion.2 = f32[320,512]{1,0:T(8,128)} fusion(f32[320,512]{1,0:T(8,128)} %fusion.8, s32[1024]{0:T(1024)} %param.24, f32[1024,1536]{1,0:T(8,128)} %fusion.28), kind=kCustom, calls=%fused_computation.8 | custom fusion | flops 524288 | bytes 2752512 | tf_op jit(solution)/shard_map/scatter-add | solution.py:112
  155.2 4.1 %slice_add_fusion = f32[1024,512]{1,0:T(8,128)} fusion(f32[1024,512]{1,0:T(8,128)} %param.16, f32[1024,1536]{1,0:T(8,128)} %fusion.28), kind=kLoop, calls=%fused_computation.7 | loop fusion | flops 524288 | bytes 6291456 | tf_op jit(solution)/shard_map/add | solution.py:110
  159.3 3.4 %reduce-scatter.9.cloned.1.call-done = f32[160,512]{1,0:T(8,128)} async-done(((f32[320,512]{1,0:T(8,128)}), f32[160,512]{1,0:T(8,128)}) %reduce-scatter.9.cloned.1.call-update) | async-done | bytes 327696 | tf_op jit(solution)/shard_map/reduce_scatter | solution.py:118
  162.7 1.8 fusion.9
  164.5 163.2 %all-reduce.3.cloned.1.call-done = (f32[768,512]{1,0:T(8,128)}, f32[256,512]{1,0:T(8,128)}, f32[512,512]{1,0:T(8,128)}, f32[256,512]{1,0:T(8,128)}) async-done(((f32[768,512]{1,0:T(8,128)}, f32[256,512]{1,0:T(8,128)}, f32[512,512]{1,0:T(8,128)}, f32[256,512]{1,0:T(8,128)}), (f32[768,512]{1,0:T(8,128)}, f32[256,512]{1,0:T(8,128)}, f32[512,512]{1,0:T(8,128)}, ...) | async-done | bytes 3670032 | tf_op jit(solution)/shard_map/psum | solution.py:126
  327.7 2.8 copy.30
  (100 shorter events, 21.7 us)
Async XLA Ops:
  7.2 28.6 %copy-start = (bf16[1536,512]{1,0:T(8,128)(2,1)S(1)}, bf16[1536,512]{1,0:T(8,128)(2,1)}, u32[]{:S(2)}) copy-start(bf16[1536,512]{1,0:T(8,128)(2,1)} %param.17) | copy-start | bytes 4718596
  7.2 57.1 %reduce-scatter.7.cloned.1.call-start = ((), (), s32[]{:S(2)}) async-start(), calls=%async_computation.6 | async-start | bytes 983040 | tf_op jit(solution)/shard_map/reduce_scatter | solution.py:97
  10.5 17.1 %collective-permute-start = (bf16[320,512]{1,0:T(8,128)(2,1)S(1)}, bf16[320,512]{1,0:T(8,128)(2,1)S(1)}, u32[]{:S(2)}, u32[]{:S(2)}) collective-permute-start(bf16[320,512]{1,0:T(8,128)(2,1)S(1)} %all_gather.6), channel_id=1, source_target_pairs={{0,2},{2,4},{4,6},{6,8},{8,10},{10,12},{12,14},{14,16},{16,18},{18... | collective-permute-start | bytes 983048 | tf_op jit(solution)/shard_map/ppermute | solution.py:16
  13.3 16.3 %collective-permute-start.1 = (bf16[320,512]{1,0:T(8,128)(2,1)S(1)}, bf16[320,512]{1,0:T(8,128)(2,1)}, u32[]{:S(2)}, u32[]{:S(2)}) collective-permute-start(bf16[320,512]{1,0:T(8,128)(2,1)S(1)} %all_gather.6), channel_id=1, source_target_pairs={{2,0},{4,2},{6,4},{8,6},{10,8},{12,10},{14,12},{16,14},{18,16},{20... | collective-permute-start | bytes 983048 | tf_op jit(solution)/shard_map/ppermute | solution.py:17
  23.1 3.4 %copy-start.21 = (s32[1024]{0:T(1024)S(1)}, s32[1024]{0:T(1024)}, u32[]{:S(2)}) copy-start(s32[1024]{0:T(1024)} %param.23) | copy-start | bytes 12292
  35.8 5.2 %copy-start.16 = (bf16[512,512]{1,0:T(8,128)(2,1)S(1)}, bf16[512,512]{1,0:T(8,128)(2,1)}, u32[]{:S(2)}) copy-start(bf16[512,512]{1,0:T(8,128)(2,1)} %param.18) | copy-start | bytes 1572868
  41.0 1.1 copy-start.12
  41.0 2.1 copy-start.20
  41.8 1.3 copy-start.1
  55.8 9.6 %copy-start.3 = (bf16[1024,512]{1,0:T(8,128)(2,1)S(1)}, bf16[1024,512]{1,0:T(8,128)(2,1)}, u32[]{:S(2)}) copy-start(bf16[1024,512]{1,0:T(8,128)(2,1)} %param.20) | copy-start | bytes 3145732
  55.8 98.7 %reduce-scatter.17.cloned.1.call-start = ((), (), s32[]{:S(2)}) async-start(), calls=%async_computation.11 | async-start | bytes 1572864 | tf_op jit(solution)/shard_map/reduce_scatter | solution.py:124
  64.3 1.4 copy-start.22
  66.8 1.4 copy-start.18
  68.2 86.4 %reduce-scatter.13.cloned.1.call-start = ((), (), s32[]{:S(2)}) async-start(), calls=%async_computation.9 | async-start | bytes 1572864 | tf_op jit(solution)/shard_map/reduce_scatter | solution.py:122
  81.3 3.6 %copy-start.2 = (f32[1024,512]{0,1:T(8,128)S(1)}, f32[1024,512]{0,1:T(8,128)}, u32[]{:S(2)}) copy-start(f32[1024,512]{0,1:T(8,128)} %copy-done.1) | copy-start | bytes 6291460
  85.0 1.2 copy-start.13
  88.0 66.6 %reduce-scatter.15.cloned.1.call-start = ((), (), s32[]{:S(2)}) async-start(), calls=%async_computation.10 | async-start | bytes 3145728 | tf_op jit(solution)/shard_map/reduce_scatter | solution.py:123
  89.8 1.0 copy-start.17
  89.8 64.8 %reduce-scatter.11.cloned.1.call-start = ((), (), s32[]{:S(2)}) async-start(), calls=%async_computation.8 | async-start | bytes 4718592 | tf_op jit(solution)/shard_map/reduce_scatter | solution.py:121
  90.8 3.9 %copy-start.8 = (bf16[1024,512]{1,0:T(8,128)(2,1)S(1)}, bf16[1024,512]{1,0:T(8,128)(2,1)}, u32[]{:S(2)}) copy-start(bf16[1024,512]{1,0:T(8,128)(2,1)} %gather_fusion.1) | copy-start | bytes 3145732
  90.8 3.9 %copy-start.9 = (bf16[1024,512]{1,0:T(8,128)(2,1)S(1)}, bf16[1024,512]{1,0:T(8,128)(2,1)}, u32[]{:S(2)}) copy-start(bf16[1024,512]{1,0:T(8,128)(2,1)} %convert_element_type.35) | copy-start | bytes 3145732
  90.8 3.9 %copy-start.10 = (bf16[1024,512]{1,0:T(8,128)(2,1)S(1)}, bf16[1024,512]{1,0:T(8,128)(2,1)}, u32[]{:S(2)}) copy-start(bf16[1024,512]{1,0:T(8,128)(2,1)} %gather_fusion) | copy-start | bytes 3145732
  98.3 1.2 copy-start.24
  98.4 64.3 %reduce-scatter.9.cloned.1.call-start = ((), (), s32[]{:S(2)}) async-start(), calls=%async_computation.7 | async-start | bytes 983040 | tf_op jit(solution)/shard_map/reduce_scatter | solution.py:118
  112.0 19.9 %collective-permute-start.2 = (f32[320,512]{1,0:T(8,128)S(1)}, f32[320,512]{1,0:T(8,128)S(1)}, u32[]{:S(2)}, u32[]{:S(2)}) collective-permute-start(f32[320,512]{1,0:T(8,128)S(1)} %get-tuple-element.15), channel_id=1, source_target_pairs={{0,30},{2,0},{4,2},{6,4},{8,6},{10,8},{12,10},{14,12},{16,14},{18,... | collective-permute-start | bytes 1966088 | tf_op jit(solution)/shard_map/ppermute | solution.py:25
  117.4 26.7 %collective-permute-start.3 = (f32[320,512]{1,0:T(8,128)S(1)}, f32[320,512]{1,0:T(8,128)S(1)}, u32[]{:S(2)}, u32[]{:S(2)}) collective-permute-start(f32[320,512]{1,0:T(8,128)S(1)} %get-tuple-element.16), channel_id=1, source_target_pairs={{0,2},{2,4},{4,6},{6,8},{8,10},{10,12},{12,14},{14,16},{16,18},{18... | collective-permute-start | bytes 1966088 | tf_op jit(solution)/shard_map/ppermute | solution.py:25
  154.4 173.3 %all-reduce.3.cloned.1.call-start = ((), (), s32[]{:S(2)}) async-start(), calls=%async_computation.12 | async-start | bytes 7340032 | tf_op jit(solution)/shard_map/psum | solution.py:126
  155.2 7.5 %copy-start.5 = (f32[160,512]{1,0:T(8,128)S(1)}, f32[160,512]{1,0:T(8,128)}, u32[]{:S(2)}) copy-start(f32[160,512]{1,0:T(8,128)} %param.15) | copy-start | bytes 983044
  155.2 7.5 %copy-start.7 = (f32[160,1024]{1,0:T(8,128)S(1)}, f32[160,1024]{1,0:T(8,128)}, u32[]{:S(2)}) copy-start(f32[160,1024]{1,0:T(8,128)} %copy-done.6) | copy-start | bytes 1966084
  327.7 2.8 copy-start.15
  327.7 3.6 %copy-start.11 = (f32[512,512]{1,0:T(8,128)S(1)}, f32[512,512]{1,0:T(8,128)}, u32[]{:S(2)}) copy-start(f32[512,512]{1,0:T(8,128)} %get-tuple-element.29) | copy-start | bytes 3145732
  330.5 1.8 copy-start.14
  (4 other events, 3.8 us)
Sparse Core Ops, SparseCore 0:
  55.9 8.3 reduce-scatter.6
  68.3 9.4 reduce-scatter.16
  88.1 9.4 reduce-scatter.12
  99.7 10.9 reduce-scatter.14
  112.8 12.4 reduce-scatter.10
  154.5 8.1 reduce-scatter.8
  168.8 158.8 all-reduce.2
where the time goes:
time: 341 us; the launch traced here: 340 us
  waiting for transfers between devices  203 us (60%)
  other arithmetic  45.5 us (13%)
  local copies, waits for them, and re-layouts  35 us (10%)
  matrix products  24.5 us (7%)
  between operations  15.1 us (4%)
  starting transfers between devices  12.5 us (4%)
  blocking collectives  4.62 us (1%)
    psum x1, waiting for transfers between devices, local(): lax.psum((pieces_w[0], pieces_w[1], pieces_w[2], pieces_w[3]), 'patch')  163 us
    ppermute x2, waiting for transfers between devices, shifted(): return lax.ppermute(value, axis, pairs)  26.7 us
    unnamed x55, local copies, waits for them, and re-layouts  14 us
    scatter-add x1, other arithmetic, local(): jax.ops.segment_sum(edge_gin[:, 2 * width:], receivers, num_segments=patc...  9.26 us
    scatter-add x1, other arithmetic, local(): jax.ops.segment_sum(edge_upd, receivers, num_segments=patch_rows)  8.07 us
    scatter-add x1, other arithmetic, local(): jax.ops.segment_sum(edge_gin[:, width:2 * width], senders, num_segments=3...  7.86 us
    gather x2, local copies, waits for them, and re-layouts, local(): edge_gupd = (edge_cot + grad_patch[receivers]) * live  7.82 us
  transfers between devices with their start and end apart: 11, of which 7 were waited for; matrix products, arithmetic and copies ran while one was open for 19% of the time, Pallas kernels for 0%

commit v1 on v0

v1 whole, which is shorter than its diff:
```python
import functools

import jax
import jax.numpy as jnp
from jax import lax
from jax.experimental import pallas as pl
from jax.experimental.pallas import tpu as pltpu
from jax.sharding import PartitionSpec as P

EPS = 1e-05
BF = jnp.bfloat16
F32 = jnp.float32
MESH = pl.DeviceIdType.MESH
VMEM = pl.BlockSpec(memory_space=pltpu.VMEM)
SMEM = pl.BlockSpec(memory_space=pltpu.SMEM)
LIMIT = 60 * 1024 * 1024


def axis_sizes(n):
    x = round((n / 2) ** (1 / 3))
    return (x, x, 2 * x) if 2 * x**3 == n else (1, 1, n)


def dot(a, b):
    return jnp.dot(a, b, preferred_element_type=F32)


def dot_tn(a, b):
    return lax.dot_general(a, b, (((0,), (0,)), ((), ())), preferred_element_type=F32)


def dot_nt(a, b):
    return lax.dot_general(a, b, (((1,), (1,)), ((), ())), preferred_element_type=F32)


def hot_rows(col, width):
    at = lax.broadcasted_iota(jnp.int32, (col.shape[0], width), 1)
    return jnp.where(at == col, 1.0, 0.0).astype(BF)


def hot_cols(row, height):
    at = lax.broadcasted_iota(jnp.int32, (height, row.shape[1]), 0)
    return jnp.where(at == row, 1.0, 0.0).astype(BF)


def mean(x):
    return jnp.mean(x, axis=-1, keepdims=True)


def mlp_tail(pre, w2):
    sig = jax.nn.sigmoid(pre)
    act = (pre * sig).astype(BF)
    slope = sig * (1.0 + pre * (1.0 - sig))
    out = dot(act, w2)
    center = out - mean(out)
    inv = lax.rsqrt(mean(center * center) + EPS)
    return act, slope, center * inv, inv


def norm_backward(grad, gain, normed, inv):
    scaled = grad * gain
    return (inv * (scaled - mean(scaled) - normed * mean(scaled * normed))).astype(BF)


def greet(peers):
    barrier = pltpu.get_barrier_semaphore()
    for peer in peers:
        pl.semaphore_signal(barrier, inc=1, device_id=peer, device_id_type=MESH)
    pl.semaphore_wait(barrier, len(peers))


def remote(src, dst, send, recv, device):
    return pltpu.make_async_remote_copy(
        src_ref=src, dst_ref=dst, send_sem=send, recv_sem=recv, device_id=device, device_id_type=MESH
    )


def comm_params(ident):
    return pltpu.CompilerParams(collective_id=ident, has_side_effects=True, vmem_limit_bytes=LIMIT)


def exchange_kernel(n, x_ref, ext_ref, send, recv, local):
    rows = x_ref.shape[0]
    p, g = lax.axis_index("patch"), lax.axis_index("grp")
    after, before = lax.rem(p + 1, n), lax.rem(p + n - 1, n)
    mate = (p, 1 - g)
    greet([mate, (after, g), (before, g)])

    def place(slab):
        return ext_ref.at[slab, g]

    own = pltpu.make_async_copy(x_ref, place(1), local)
    to_after = remote(x_ref, place(0), send.at[0], recv.at[0], (after, g))
    to_before = remote(x_ref, place(2), send.at[1], recv.at[1], (before, g))
    to_mate = remote(x_ref, place(1), send.at[2], recv.at[2], mate)
    to_after.start()
    to_before.start()
    to_mate.start()
    own.start()
    to_after.wait_recv()
    pass_0 = remote(place(0), place(0), send.at[3], recv.at[3], mate)
    pass_0.start()
    to_before.wait_recv()
    pass_2 = remote(place(2), place(2), send.at[4], recv.at[4], mate)
    pass_2.start()
    own.wait()
    to_mate.wait()
    pass_0.wait()
    pass_2.wait()
    to_after.wait_send()
    to_before.wait_send()


def exchange(node_bf, n):
    rows, d = node_bf.shape
    return pl.pallas_call(
        functools.partial(exchange_kernel, n),
        out_shape=jax.ShapeDtypeStruct((3, 2, rows, d), BF),
        in_specs=[VMEM],
        out_specs=VMEM,
        scratch_shapes=[
            pltpu.SemaphoreType.DMA((5,)),
            pltpu.SemaphoreType.DMA((5,)),
            pltpu.SemaphoreType.DMA,
        ],
        compiler_params=comm_params(0),
        name="node_exchange",
    )(node_bf)


def forward_kernel(
    count, el, ext, snd_c, rcv_c, rcv_r, w1, w2, gain, act_o, slope_o, normed_o, inv_o, agg_o, agg
):
    i = pl.program_id(0)
    tile, d = el.shape
    nodes = agg.shape[0]
    x_s = dot(hot_rows(snd_c[...], 3 * nodes), ext[...]).astype(BF)
    x_r = dot(hot_rows(rcv_c[...], nodes), ext[nodes : 2 * nodes, :]).astype(BF)
    pre = dot(el[...].astype(BF), w1[0:d, :])
    pre += dot(x_s, w1[d : 2 * d, :])
    pre += dot(x_r, w1[2 * d : 3 * d, :])
    act, slope, normed, inv = mlp_tail(pre, w2[...])
    act_o[...] = act
    slope_o[...] = slope.astype(BF)
    normed_o[...] = normed.astype(BF)
    inv_o[...] = inv
    slot = i * tile + lax.broadcasted_iota(jnp.int32, (tile, 1), 0)
    upd = jnp.where(slot < count[0], normed * gain[...], 0.0).astype(BF)
    part = dot(hot_cols(rcv_r[...], nodes), upd)

    @pl.when(i == 0)
    def _():
        agg[...] = part

    @pl.when(i > 0)
    def _():
        agg[...] += part

    @pl.when(i == pl.num_programs(0) - 1)
    def _():
        agg_o[...] = agg[...].astype(BF)


def whole(shape):
    return pl.BlockSpec(shape, lambda i: (0, 0), pipeline_mode=pl.Buffered(1))


def edge_forward(count, el, ext, snd_c, rcv_c, rcv_r, w1, w2, gain, tiles):
    edges, d = el.shape
    nodes = ext.shape[0] // 3
    tile = edges // tiles

    def rows(width):
        return pl.BlockSpec((tile, width), lambda i: (i, 0))

    return pl.pallas_call(
        forward_kernel,
        grid=(tiles,),
        out_shape=(
            jax.ShapeDtypeStruct((edges, d), BF),
            jax.ShapeDtypeStruct((edges, d), BF),
            jax.ShapeDtypeStruct((edges, d), BF),
            jax.ShapeDtypeStruct((edges, 1), F32),
            jax.ShapeDtypeStruct((nodes, d), BF),
        ),
        in_specs=[
            SMEM,
            rows(d),
            whole(ext.shape),
            rows(1),
            rows(1),
            pl.BlockSpec((1, tile), lambda i: (0, i)),
            whole(w1.shape),
            whole(w2.shape),
            whole(gain.shape),
        ],
        out_specs=(rows(d), rows(d), rows(d), rows(1), whole((nodes, d))),
        scratch_shapes=[pltpu.VMEM((nodes, d), F32)],
        compiler_params=pltpu.CompilerParams(
            dimension_semantics=("arbitrary",), vmem_limit_bytes=LIMIT
        ),
        name="edge_forward",
    )(count, el, ext, snd_c, rcv_c, rcv_r, w1, w2, gain)


def node_kernel(
    agg, lat, cot, w1, w2, gain, gagg_o, part_o, dw1_o, dw2_o, other, mine, send, recv, local
):
    p, g = lax.axis_index("patch"), lax.axis_index("grp")
    mate = (p, 1 - g)
    d = lat.shape[1]
    greet([mate])
    swap = remote(agg.at[1 - g], other, send.at[0], recv.at[0], mate)
    swap.start()
    lat_bf = lat[...].astype(BF)
    pre = dot(lat_bf, w1[0:d, :])
    swap.wait()
    agg_bf = (agg[g].astype(F32) + other[...].astype(F32)).astype(BF)
    pre += dot(agg_bf, w1[d : 2 * d, :])
    act, slope, normed, inv = mlp_tail(pre, w2[...])
    gout = norm_backward(cot[...], gain[...], normed, inv)
    gpre = (dot_nt(gout, w2[...]) * slope).astype(BF)
    mine[...] = dot_nt(gpre, w1[d : 2 * d, :]).astype(BF)
    keep = pltpu.make_async_copy(mine, gagg_o.at[g], local)
    keep.start()
    give = remote(mine, gagg_o.at[g], send.at[1], recv.at[1], mate)
    give.start()
    part_o[...] = cot[...] + dot_nt(gpre, w1[0:d, :])
    dw2_o[...] = dot_tn(act, gout).astype(BF)
    dw1_o[0:d, :] = dot_tn(lat_bf, gpre).astype(BF)
    dw1_o[d : 2 * d, :] = dot_tn(agg_bf, gpre).astype(BF)
    keep.wait()
    give.wait()


def node_layer(agg, lat, cot, w1, w2, gain):
    rows, d = lat.shape
    return pl.pallas_call(
        node_kernel,
        out_shape=(
            jax.ShapeDtypeStruct((2, rows, d), BF),
            jax.ShapeDtypeStruct((rows, d), F32),
            jax.ShapeDtypeStruct(w1.shape, BF),
            jax.ShapeDtypeStruct(w2.shape, BF),
        ),
        in_specs=[VMEM] * 6,
        out_specs=(VMEM,) * 4,
        scratch_shapes=[
            pltpu.VMEM((rows, d), BF),
            pltpu.VMEM((rows, d), BF),
            pltpu.SemaphoreType.DMA((2,)),
            pltpu.SemaphoreType.DMA((2,)),
            pltpu.SemaphoreType.DMA,
        ],
        compiler_params=comm_params(1),
        name="node_layer",
    )(agg, lat, cot, w1, w2, gain)


def backward_kernel(
    count, el, ec, act, slope, normed, inv, gagg, ext, snd_r, rcv_c, rcv_r, w1, w2, gain,
    grad_o, sent_o, dw1_o, dw2_o, by_s, by_r, dwe, dw2,
):
    i = pl.program_id(0)
    tile, d = el.shape
    nodes = gagg.shape[0]

    @pl.when(i == 0)
    def _():
        by_s[...] = jnp.zeros_like(by_s)
        by_r[...] = jnp.zeros_like(by_r)
        dwe[...] = jnp.zeros_like(dwe)
        dw2[...] = jnp.zeros_like(dw2)

    slot = i * tile + lax.broadcasted_iota(jnp.int32, (tile, 1), 0)
    back = dot(hot_rows(rcv_c[...], nodes), gagg[...])
    gupd = jnp.where(slot < count[0], ec[...] + back, 0.0)
    gout = norm_backward(gupd, gain[...], normed[...].astype(F32), inv[...])
    gpre = (dot_nt(gout, w2[...]) * slope[...].astype(F32)).astype(BF)
    grad_o[...] = ec[...] + dot_nt(gpre, w1[0:d, :])
    dw2[...] += dot_tn(act[...], gout)
    dwe[...] += dot_tn(el[...].astype(BF), gpre)
    by_s[...] += dot(hot_cols(snd_r[...], 3 * nodes), gpre)
    by_r[...] += dot(hot_cols(rcv_r[...], nodes), gpre)

    @pl.when(i == pl.num_programs(0) - 1)
    def _():
        dw2_o[...] = dw2[...].astype(BF)
        dw1_o[0:d, :] = dwe[...].astype(BF)
        s_bf = by_s[...].astype(BF)
        r_bf = by_r[...].astype(BF)
        dw1_o[d : 2 * d, :] = dot_tn(ext[...], s_bf).astype(BF)
        dw1_o[2 * d : 3 * d, :] = dot_tn(ext[nodes : 2 * nodes, :], r_bf).astype(BF)
        spread = dot_nt(s_bf, w1[d : 2 * d, :])
        sent_o[0:nodes, :] = spread[0:nodes].astype(BF)
        kept = spread[nodes : 2 * nodes] + dot_nt(r_bf, w1[2 * d : 3 * d, :])
        sent_o[nodes : 2 * nodes, :] = kept.astype(BF)
        sent_o[2 * nodes : 3 * nodes, :] = spread[2 * nodes : 3 * nodes].astype(BF)


def edge_backward(
    count, el, ec, act, slope, normed, inv, gagg, ext, snd_r, rcv_c, rcv_r, w1, w2, gain, tiles
):
    edges, d = el.shape
    nodes = gagg.shape[0]
    tile = edges // tiles

    def rows(width):
        return pl.BlockSpec((tile, width), lambda i: (i, 0))

    line = pl.BlockSpec((1, tile), lambda i: (0, i))
    return pl.pallas_call(
        backward_kernel,
        grid=(tiles,),
        out_shape=(
            jax.ShapeDtypeStruct((edges, d), F32),
            jax.ShapeDtypeStruct((3 * nodes, d), BF),
            jax.ShapeDtypeStruct(w1.shape, BF),
            jax.ShapeDtypeStruct(w2.shape, BF),
        ),
        in_specs=[
            SMEM, rows(d), rows(d), rows(d), rows(d), rows(d), rows(1),
            whole(gagg.shape), whole(ext.shape), line, rows(1), line,
            whole(w1.shape), whole(w2.shape), whole(gain.shape),
        ],
        out_specs=(rows(d), whole((3 * nodes, d)), whole(w1.shape), whole(w2.shape)),
        scratch_shapes=[
            pltpu.VMEM((3 * nodes, d), F32),
            pltpu.VMEM((nodes, d), F32),
            pltpu.VMEM((d, d), F32),
            pltpu.VMEM((d, d), F32),
        ],
        compiler_params=pltpu.CompilerParams(
            dimension_semantics=("arbitrary",), vmem_limit_bytes=LIMIT
        ),
        name="edge_backward",
    )(count, el, ec, act, slope, normed, inv, gagg, ext, snd_r, rcv_c, rcv_r, w1, w2, gain)


def plan_of(rows, sizes, order):
    steps = []
    for axis in order:
        n = sizes[axis]
        if n > 1:
            left = rows // n if rows % (16 * n) == 0 else rows
            steps.append((axis, n, rows, left))
            rows = left
    return steps


def reduce_kernel(n, plans, widths, names, *refs):
    sent, d_e1, d_e2, d_n1, d_n2, share_o = refs[:6]
    outs = refs[6:8]
    rest = dict(zip(names, refs[8:]))
    p, g = lax.axis_index("patch"), lax.axis_index("grp")
    nx, ny, nz = axis_sizes(n)
    here = (lax.rem(p, nx), lax.rem(p // nx, ny), p // (nx * ny))
    sizes, strides = (nx, ny, nz), (1, nx, nx * ny)
    after, before = lax.rem(p + 1, n), lax.rem(p + n - 1, n)
    mate = (p, 1 - g)

    def along(axis, step):
        c = here[axis]
        t = lax.rem(c + step, sizes[axis])
        return t, (p + (t - c) * strides[axis], g)

    peers = [mate, (after, g), (before, g)]
    for axis in range(3):
        peers += [along(axis, step)[1] for step in range(1, sizes[axis])]
    greet(peers)
    send, recv = rest["send"], rest["recv"]
    used = [0]
    pending = []

    def go(src, dst, device):
        k = used[0]
        used[0] += 1
        copy = remote(src, dst, send.at[k], recv.at[k], device)
        copy.start()
        pending.append(copy)
        return copy

    def window(ref, start, size, cols):
        if not isinstance(start, int):
            start = pl.multiple_of(start, 16)
        return ref.at[pl.ds(start, size), cols]

    halves = ((d_n1, d_n2), (d_e2, d_e1))
    first = []
    for s in range(2):
        got, at = [], 0
        for part in halves[s]:
            size = part.shape[1]
            got.append((go(part.at[1 - g], rest[f"in{s}"].at[pl.ds(at, size)], mate), part, at, size))
            at += size
        first.append(got)
        if s == 0:
            nodes_in = [go(sent.at[k, 1 - g], rest["sin"].at[k], mate) for k in range(3)]

    def start_reduce(s, c, k):
        axis, m, r, left = plans[s][c][k]
        cols = pl.ds(c * widths, widths)
        flow = []
        for step in range(1, m):
            t, device = along(axis, step)
            if k == 0:
                base = rest[f"cur{s}"]
                src = window(base, t * left if left < r else 0, left, cols)
            else:
                base = rest[f"acc{s}_{c}_{k - 1}"]
                src = window(base, t * left if left < r else 0, left, pl.ds(0, widths))
            flow.append(go(src, rest[f"rx{s}_{c}_{k}"].at[step - 1], device))
        return flow

    def finish_reduce(s, c, k, flow):
        axis, m, r, left = plans[s][c][k]
        mine = here[axis] * left if left < r else 0
        for copy in flow:
            copy.wait_recv()
        if k == 0:
            own = window(rest[f"cur{s}"], mine, left, pl.ds(c * widths, widths))
        else:
            own = window(rest[f"acc{s}_{c}_{k - 1}"], mine, left, pl.ds(0, widths))
        total = own[...].astype(F32)
        for step in range(m - 1):
            total += rest[f"rx{s}_{c}_{k}"][step].astype(F32)
        return total.astype(BF)

    def offset(s, c, depth):
        at = 0
        for axis, m, r, left in plans[s][c][:depth]:
            if left < r:
                at = at + here[axis] * left
        return at

    def start_gather(s, c, k):
        axis, m, r, left = plans[s][c][k]
        if left == r:
            return []
        cols = pl.ds(c * widths, widths)
        block = window(outs[s], offset(s, c, k + 1), left, cols)
        return [go(block, block, along(axis, step)[1]) for step in range(1, m)]

    flows = {}
    depth = len(plans[0][0])
    for s in range(2):
        cur = rest[f"cur{s}"]
        for copy, part, at, size in first[s]:
            copy.wait_recv()
            cur[at : at + size, :] = (
                part[g].astype(F32) + rest[f"in{s}"][at : at + size, :].astype(F32)
            ).astype(BF)
        for c in range(2):
            flows[s, c] = start_reduce(s, c, 0)
        if s == 0:
            for copy in nodes_in:
                copy.wait_recv()
            home = rest["home"]
            total = sent[:, g].astype(F32) + rest["sin"][...].astype(F32)
            home[...] = total.astype(BF)
            share = total[1]
            back = go(home.at[0], rest["from"].at[0], (before, g))
            forth = go(home.at[2], rest["from"].at[1], (after, g))
    for k in range(depth):
        for s in range(2):
            for c in range(2):
                total = finish_reduce(s, c, k, flows[s, c])
                if k < depth - 1:
                    rest[f"acc{s}_{c}_{k}"][...] = total
                    flows[s, c] = start_reduce(s, c, k + 1)
                else:
                    block = window(
                        outs[s], offset(s, c, depth), plans[s][c][k][3], pl.ds(c * widths, widths)
                    )
                    block[...] = total
                    flows[s, c] = start_gather(s, c, k)
    back.wait_recv()
    forth.wait_recv()
    share_o[...] = (
        rest["home"][1].astype(F32) + rest["from"][0].astype(F32) + rest["from"][1].astype(F32)
    )
    for k in range(depth - 1, -1, -1):
        for s in range(2):
            for c in range(2):
                for copy in flows[s, c]:
                    copy.wait_recv()
                if k > 0:
                    flows[s, c] = start_gather(s, c, k - 1)
    for copy in pending:
        copy.wait_send()


def reduce_all(n, sent, d_e1, d_e2, d_n1, d_n2):
    d = sent.shape[-1]
    rows = sent.shape[2]
    sizes = axis_sizes(n)
    totals = (d_n1.shape[1] + d_n2.shape[1], d_e2.shape[1] + d_e1.shape[1])
    orders = ((0, 1, 2), (1, 0, 2))
    plans = [[plan_of(total, sizes, order) for order in orders] for total in totals]
    wide = d // 2
    scratch = {
        "sin": pltpu.VMEM((3, rows, d), BF),
        "home": pltpu.VMEM((3, rows, d), BF),
        "from": pltpu.VMEM((2, rows, d), BF),
    }
    copies = 4 + 3 + 2
    for s in range(2):
        scratch[f"in{s}"] = pltpu.VMEM((totals[s], d), BF)
        scratch[f"cur{s}"] = pltpu.VMEM((totals[s], d), BF)
        for c in range(2):
            for k, (axis, m, r, left) in enumerate(plans[s][c]):
                scratch[f"rx{s}_{c}_{k}"] = pltpu.VMEM((m - 1, left, wide), BF)
                scratch[f"acc{s}_{c}_{k}"] = pltpu.VMEM((left, wide), BF)
                copies += 2 * (m - 1)
    scratch["send"] = pltpu.SemaphoreType.DMA((copies,))
    scratch["recv"] = pltpu.SemaphoreType.DMA((copies,))
    return pl.pallas_call(
        functools.partial(reduce_kernel, n, plans, wide, tuple(scratch)),
        out_shape=(
            jax.ShapeDtypeStruct((rows, d), F32),
            jax.ShapeDtypeStruct((totals[0], d), BF),
            jax.ShapeDtypeStruct((totals[1], d), BF),
        ),
        in_specs=[VMEM] * 5,
        out_specs=(VMEM,) * 3,
        scratch_shapes=list(scratch.values()),
        compiler_params=comm_params(2),
        name="reduce_all",
    )(sent, d_e1, d_e2, d_n1, d_n2)


def local(
    node_latent,
    edge_latent,
    node_cot,
    edge_cot,
    edge_w1,
    edge_w2,
    edge_gain,
    node_w1,
    node_w2,
    node_gain,
    senders,
    receivers,
    counts,
):
    n = lax.axis_size("patch")
    rows, d = node_latent.shape
    edges = edge_latent.shape[0]
    tiles = 4
    ext = exchange(node_latent.astype(BF), n).reshape(6 * rows, d)
    snd_c, rcv_c = senders.reshape(edges, 1), receivers.reshape(edges, 1)
    snd_r, rcv_r = senders.reshape(1, edges), receivers.reshape(1, edges)
    e_gain, n_gain = edge_gain.reshape(1, d), node_gain.reshape(1, d)
    act, slope, normed, inv, agg = edge_forward(
        counts, edge_latent, ext, snd_c, rcv_c, rcv_r, edge_w1, edge_w2, e_gain, tiles
    )
    gagg, part, d_n1, d_n2 = node_layer(
        agg.reshape(2, rows, d), node_latent, node_cot, node_w1, node_w2, n_gain
    )
    edge_grad, sent, d_e1, d_e2 = edge_backward(
        counts, edge_latent, edge_cot, act, slope, normed, inv, gagg.reshape(2 * rows, d), ext,
        snd_r, rcv_c, rcv_r, edge_w1, edge_w2, e_gain, tiles,
    )

    def halves(x):
        return x.reshape(2, x.shape[0] // 2, d)

    share, node_sum, edge_sum = reduce_all(
        n, sent.reshape(3, 2, rows, d), halves(d_e1), halves(d_e2), halves(d_n1), halves(d_n2)
    )
    cut_n, cut_e = node_w1.shape[0] // 2, edge_w2.shape[0] // 2
    return (
        part + share,
        edge_grad,
        edge_sum[cut_e:].astype(F32),
        edge_sum[:cut_e].astype(F32),
        node_sum[:cut_n].astype(F32),
        node_sum[cut_n:].astype(F32),
    )


def solution(mesh):
    line = P(("patch", "grp"))
    block = P(("patch", "grp"), None)
    in_specs = (block,) * 4 + (P(),) * 6 + (line,) * 3
    out_specs = (block, block) + (P("grp", None),) * 4
    return jax.shard_map(local, mesh=mesh, in_specs=in_specs, out_specs=out_specs, check_vma=False)
```

time: 341 us -> 125 us (0.37)
  waiting for transfers between devices: 203 us -> 0 us
  Pallas kernels: 0 us -> 110 us
  other arithmetic: 45.5 us -> 9.04 us
  local copies, waits for them, and re-layouts: 35 us -> 3.42 us
  matrix products: 24.5 us -> 0 us
  between operations: 15.1 us -> 1.34 us
  starting transfers between devices: 12.5 us -> 0 us
  blocking collectives: 4.62 us -> 0 us
    psum x1 -> x0, waiting for transfers between devices: 163 us -> none  [local(): lax.psum((pieces_w[0], pieces_w[1], pieces_w[2], pieces_w[3]), 'patch')]
    pallas_call x0 -> x5, Pallas kernels: none -> 110 us  [the longest x1 64 us: reduce_all(): pl.pallas_call(functools.partial(reduce_kernel, n, plans, wide, tuple(scr...]
    ppermute x4 -> x0, waiting for transfers between devices: 29.8 us -> none  [the longest x2 26.7 us: shifted(): return lax.ppermute(value, axis, pairs)]
    scatter-add x3 -> x0, other arithmetic: 25.2 us -> none  [the longest x1 9.26 us: local(): jax.ops.segment_sum(edge_gin[:, 2 * width:], receivers, num_segments=patc...]
    dot_general x12 -> x0, matrix products: 24.5 us -> none  [the longest x2 5.56 us: mlp_forward(): pre = jnp.dot(inputs, first, preferred_element_type=jnp.float32)]
    gather x4 -> x0, local copies, waits for them, and re-layouts: 18 us -> none  [the longest x2 7.82 us: local(): edge_gupd = (edge_cot + grad_patch[receivers]) * live]
    unnamed x55 -> x4, local copies, waits for them, and re-layouts: 14 us -> 0.01 us
    ppermute x4 -> x0, starting transfers between devices: 12.2 us -> none  [the longest x2 5.4 us: shifted(): return lax.ppermute(value, axis, pairs)]
  transfers between devices with their start and end apart: 11 -> 0, of which waited for: 7 -> 0; matrix products, arithmetic and copies ran while one was open for 19% -> 0% of each run, Pallas kernels for 0% -> 0%
where the time goes in v1:
time: 125 us; the launch traced here: 124 us
  Pallas kernels  110 us (88%)
  other arithmetic  9.04 us (7%)
  local copies, waits for them, and re-layouts  3.42 us (3%)
  between operations  1.34 us (1%)
    pallas_call x1, Pallas kernels, reduce_all(): pl.pallas_call(functools.partial(reduce_kernel, n, plans, wide, tuple(scr...  64 us
    pallas_call x1, Pallas kernels, exchange(): pl.pallas_call(functools.partial(exchange_kernel, n), out_shape=jax.Shape...  15.2 us
    pallas_call x1, Pallas kernels, edge_backward(): pl.pallas_call(backward_kernel, grid=(tiles,), out_shape=(jax.ShapeDtypeS...  13.5 us
    pallas_call x1, Pallas kernels, edge_forward(): pl.pallas_call(forward_kernel, grid=(tiles,), out_shape=(jax.ShapeDtypeSt...  10.6 us
    pallas_call x1, Pallas kernels, node_layer(): pl.pallas_call(node_kernel, out_shape=(jax.ShapeDtypeStruct((2, rows, d),...  7.31 us
    reshape x2, local copies, waits for them, and re-layouts, local(): snd_c, rcv_c = (senders.reshape(edges, 1), receivers.reshape(edges, 1))  3.41 us

profile of v1, /device:TPU:0, one launch (start us, length us, event | category | flops | bytes accessed | tf_op | source)
XLA Modules:
  0.0 124.3 jit_solution(2780090447764030476)
XLA Ops:
  1.3 1.7 %convert_element_type.15.x_ref = bf16[160,512]{1,0:T(8,128)(2,1)} convert(f32[160,512]{1,0:T(8,128)} %lat.1) | non-fusion elementwise | flops 81920 | bytes 491520 | tf_op jit(solution)/shard_map/convert_element_type | solution.py:551
  2.9 1.7 %copy.20.rcv_c = s32[1024,1]{1,0:T(8,128)} copy(s32[1024,1]{0,1:T(1,128)} %bitcast.23) | data formatting | bytes 8192 | tf_op jit(solution)/shard_map/reshape | solution.py:552
  4.6 1.7 %copy.19.snd_c = s32[1024,1]{1,0:T(8,128)} copy(s32[1024,1]{0,1:T(1,128)} %bitcast.26) | data formatting | bytes 8192 | tf_op jit(solution)/shard_map/reshape | solution.py:552
  6.4 15.2 %node_exchange.1 = bf16[3,2,160,512]{3,2,1,0:T(8,128)(2,1)} custom-call(bf16[160,512]{1,0:T(8,128)(2,1)} %convert_element_type.15.x_ref), custom_call_target="tpu_custom_call" | custom-call | tf_op jit(solution)/shard_map/node_exchange/pallas_call | solution.py:116
  21.5 10.6 %edge_forward.1 = (bf16[1024,512]{1,0:T(8,128)(2,1)}, bf16[1024,512]{1,0:T(8,128)(2,1)}, bf16[1024,512]{1,0:T(8,128)(2,1)}, f32[1024,1]{1,0:T(8,128)}, bf16[320,512]{1,0:T(8,128)(2,1)}) custom-call(s32[1]{0:T(128)S(6)} %copy.22.count, f32[1024,512]{1,0:T(8,128)} %el.3, bf16[960,512]{1,0:T(8,128)(2,1)} %bitcast.14, s32[1024,1]{1,0:T(8,128)} %copy.19.snd_c, ...), custom_call_target="tpu_custom_call" | custom-call | tf_op jit(solution)/shard_map/edge_forward/pallas_call | solution.py:176
  32.1 7.3 %node_layer.1 = (bf16[2,160,512]{2,1,0:T(8,128)(2,1)}, f32[160,512]{1,0:T(8,128)}, bf16[1024,512]{1,0:T(8,128)(2,1)}, bf16[512,512]{1,0:T(8,128)(2,1)}) custom-call(bf16[2,160,512]{2,1,0:T(8,128)(2,1)} %bitcast.22, f32[160,512]{1,0:T(8,128)} %lat.1, f32[160,512]{1,0:T(8,128)} %cot.1, bf16[1024,512]{1,0:T(8,128)(2,1)} %w1.4, bf16[512,512]{1,0:T(8,128)(2,1)} %w2.4, ...), custom_call_target="tpu_custom_call" | custom-call | tf_op jit(solution)/shard_map/node_layer/pallas_call | solution.py:238
  39.4 13.5 %edge_backward.1 = (f32[1024,512]{1,0:T(8,128)}, bf16[960,512]{1,0:T(8,128)(2,1)}, bf16[1536,512]{1,0:T(8,128)(2,1)}, bf16[512,512]{1,0:T(8,128)(2,1)}) custom-call(s32[1]{0:T(128)S(6)} %copy.22.count, f32[1024,512]{1,0:T(8,128)} %el.3, f32[1024,512]{1,0:T(8,128)} %ec.1, bf16[1024,512]{1,0:T(8,128)(2,1)} %get-tuple-element.24.act, ...), custom_call_target="tpu_custom_call" | custom-call | tf_op jit(solution)/shard_map/edge_backward/pallas_call | solution.py:312
  52.9 0.0 copy-start.1
  52.9 64.0 %reduce_all.1 = (f32[160,512]{1,0:T(8,128)}, bf16[768,512]{1,0:T(8,128)(2,1)}, bf16[1024,512]{1,0:T(8,128)(2,1)}) custom-call(bf16[3,2,160,512]{3,2,1,0:T(8,128)(2,1)} %bitcast.18, bf16[2,768,512]{2,1,0:T(8,128)(2,1)} %bitcast.16, bf16[2,256,512]{2,1,0:T(8,128)(2,1)} %bitcast.20, bf16[2,512,512]{2,1,0:T(8,128)(2,1)} %bitcast.17, bf16[2,256,512]{2,1,0:T(8,128)(2,1)} %bitcast.19), custom_call_target="tpu_custom_call" | custom-call | tf_op jit(solution)/shard_map/reduce_all/pallas_call | solution.py:517
  116.9 0.0 copy-start
  116.9 0.0 copy-done.1
  116.9 1.8 %add.3 = f32[160,512]{1,0:T(8,128)} add(f32[160,512]{1,0:T(8,128)S(1)} %copy-done.1, f32[160,512]{1,0:T(8,128)} %get-tuple-element.34) | non-fusion elementwise | flops 81920 | bytes 983040 | tf_op jit(solution)/shard_map/add | solution.py:574
  118.7 2.1 %slice_convert_fusion.1 = f32[512,512]{1,0:T(8,128)} fusion(bf16[768,512]{1,0:T(8,128)(2,1)} %get-tuple-element.37), kind=kLoop, calls=%fused_computation.1 | loop fusion | flops 262144 | bytes 1572864 | tf_op jit(solution)/shard_map/convert_element_type | solution.py:578
  120.9 0.0 copy-done
  120.9 2.0 %slice_convert_fusion.2 = (f32[256,512]{1,0:T(8,128)}, f32[256,512]{1,0:T(8,128)}) fusion(bf16[768,512]{1,0:T(8,128)(2,1)} %get-tuple-element.37, bf16[1024,512]{1,0:T(8,128)(2,1)S(1)} %copy-done), kind=kLoop, calls=%fused_computation.2 | loop fusion | flops 262144 | bytes 1572864 | tf_op jit(solution)/shard_map/convert_element_type | solution.py:579
  122.9 1.4 %slice_convert_fusion = f32[768,512]{1,0:T(8,128)} fusion(bf16[1024,512]{1,0:T(8,128)(2,1)S(1)} %copy-done), kind=kLoop, calls=%fused_computation | loop fusion | flops 393216 | bytes 2359296 | tf_op jit(solution)/shard_map/convert_element_type | solution.py:576
Async XLA Ops:
  52.9 64.0 %copy-start.1 = (f32[160,512]{1,0:T(8,128)S(1)}, f32[160,512]{1,0:T(8,128)}, u32[]{:S(2)}) copy-start(f32[160,512]{1,0:T(8,128)} %get-tuple-element.23) | copy-start | bytes 983044
  116.9 4.0 %copy-start = (bf16[1024,512]{1,0:T(8,128)(2,1)S(1)}, bf16[1024,512]{1,0:T(8,128)(2,1)}, u32[]{:S(2)}) copy-start(bf16[1024,512]{1,0:T(8,128)(2,1)} %get-tuple-element.36) | copy-start | bytes 3145732

commit v2 on v1

v2 whole, which is shorter than its diff:
```python
import functools

import jax
import jax.numpy as jnp
from jax import lax
from jax.experimental import pallas as pl
from jax.experimental.pallas import tpu as pltpu
from jax.sharding import PartitionSpec as P

EPS = 1e-05
BF = jnp.bfloat16
F32 = jnp.float32
MESH = pl.DeviceIdType.MESH
VMEM = pl.BlockSpec(memory_space=pltpu.VMEM)
SMEM = pl.BlockSpec(memory_space=pltpu.SMEM)
LIMIT = 60 * 1024 * 1024


def axis_sizes(n):
    x = round((n / 2) ** (1 / 3))
    return (x, x, 2 * x) if 2 * x**3 == n else (1, 1, n)


def dot(a, b):
    return jnp.dot(a, b, preferred_element_type=F32)


def dot_tn(a, b):
    return lax.dot_general(a, b, (((0,), (0,)), ((), ())), preferred_element_type=F32)


def dot_nt(a, b):
    return lax.dot_general(a, b, (((1,), (1,)), ((), ())), preferred_element_type=F32)


def hot_rows(col, width):
    at = lax.broadcasted_iota(jnp.int32, (col.shape[0], width), 1)
    return jnp.where(at == col, 1.0, 0.0).astype(BF)


def hot_cols(row, height):
    at = lax.broadcasted_iota(jnp.int32, (height, row.shape[1]), 0)
    return jnp.where(at == row, 1.0, 0.0).astype(BF)


def column(row):
    return jnp.transpose(jnp.broadcast_to(row, (128, row.shape[1])))[:, 0:1]


def mean(x):
    return jnp.mean(x, axis=-1, keepdims=True)


def mlp_tail(pre, w2):
    sig = jax.nn.sigmoid(pre)
    act = (pre * sig).astype(BF)
    slope = sig * (1.0 + pre * (1.0 - sig))
    out = dot(act, w2)
    center = out - mean(out)
    inv = lax.rsqrt(mean(center * center) + EPS)
    return act, slope, center * inv, inv


def norm_backward(grad, gain, normed, inv):
    scaled = grad * gain
    return (inv * (scaled - mean(scaled) - normed * mean(scaled * normed))).astype(BF)


def greet(peers):
    barrier = pltpu.get_barrier_semaphore()
    for peer in peers:
        pl.semaphore_signal(barrier, inc=1, device_id=peer, device_id_type=MESH)
    pl.semaphore_wait(barrier, len(peers))


def remote(src, dst, send, recv, device):
    return pltpu.make_async_remote_copy(
        src_ref=src, dst_ref=dst, send_sem=send, recv_sem=recv, device_id=device, device_id_type=MESH
    )


def comm_params(ident):
    return pltpu.CompilerParams(collective_id=ident, has_side_effects=True, vmem_limit_bytes=LIMIT)


def exchange_kernel(n, lat_ref, ext_ref, x_ref, send, recv, local):
    x_ref[...] = lat_ref[...].astype(BF)
    p, g = lax.axis_index("patch"), lax.axis_index("grp")
    after, before = lax.rem(p + 1, n), lax.rem(p + n - 1, n)
    mate = (p, 1 - g)
    greet([mate, (after, g), (before, g)])

    def place(slab):
        return ext_ref.at[slab, g]

    own = pltpu.make_async_copy(x_ref, place(1), local)
    to_after = remote(x_ref, place(0), send.at[0], recv.at[0], (after, g))
    to_before = remote(x_ref, place(2), send.at[1], recv.at[1], (before, g))
    to_mate = remote(x_ref, place(1), send.at[2], recv.at[2], mate)
    to_after.start()
    to_before.start()
    to_mate.start()
    own.start()
    to_after.wait_recv()
    pass_0 = remote(place(0), place(0), send.at[3], recv.at[3], mate)
    pass_0.start()
    to_before.wait_recv()
    pass_2 = remote(place(2), place(2), send.at[4], recv.at[4], mate)
    pass_2.start()
    own.wait()
    to_mate.wait()
    pass_0.wait()
    pass_2.wait()
    to_after.wait_send()
    to_before.wait_send()


def exchange(latent, n):
    rows, d = latent.shape
    return pl.pallas_call(
        functools.partial(exchange_kernel, n),
        out_shape=jax.ShapeDtypeStruct((3, 2, rows, d), BF),
        in_specs=[VMEM],
        out_specs=VMEM,
        scratch_shapes=[
            pltpu.VMEM((rows, d), BF),
            pltpu.SemaphoreType.DMA((5,)),
            pltpu.SemaphoreType.DMA((5,)),
            pltpu.SemaphoreType.DMA,
        ],
        compiler_params=comm_params(0),
        name="node_exchange",
    )(latent)


def forward_kernel(
    count, el, ext, snd_r, rcv_r, w1, w2, gain, act_o, slope_o, normed_o, inv_o, agg_o, agg
):
    i = pl.program_id(0)
    tile, d = el.shape
    nodes = agg.shape[0]
    x_s = dot(hot_rows(column(snd_r[...]), 3 * nodes), ext[...]).astype(BF)
    x_r = dot(hot_rows(column(rcv_r[...]), nodes), ext[nodes : 2 * nodes, :]).astype(BF)
    pre = dot(el[...].astype(BF), w1[0:d, :])
    pre += dot(x_s, w1[d : 2 * d, :])
    pre += dot(x_r, w1[2 * d : 3 * d, :])
    act, slope, normed, inv = mlp_tail(pre, w2[...])
    act_o[...] = act
    slope_o[...] = slope.astype(BF)
    normed_o[...] = normed.astype(BF)
    inv_o[...] = inv
    slot = i * tile + lax.broadcasted_iota(jnp.int32, (tile, 1), 0)
    upd = jnp.where(slot < count[0], normed * gain[...], 0.0).astype(BF)
    part = dot(hot_cols(rcv_r[...], nodes), upd)

    @pl.when(i == 0)
    def _():
        agg[...] = part

    @pl.when(i > 0)
    def _():
        agg[...] += part

    @pl.when(i == pl.num_programs(0) - 1)
    def _():
        agg_o[...] = agg[...].astype(BF)


def whole(shape):
    return pl.BlockSpec(shape, lambda i: (0, 0), pipeline_mode=pl.Buffered(1))


def edge_forward(count, el, ext, snd_r, rcv_r, w1, w2, gain, tiles):
    edges, d = el.shape
    nodes = ext.shape[0] // 3
    tile = edges // tiles

    def rows(width):
        return pl.BlockSpec((tile, width), lambda i: (i, 0))

    line = pl.BlockSpec((1, tile), lambda i: (0, i))
    return pl.pallas_call(
        forward_kernel,
        grid=(tiles,),
        out_shape=(
            jax.ShapeDtypeStruct((edges, d), BF),
            jax.ShapeDtypeStruct((edges, d), BF),
            jax.ShapeDtypeStruct((edges, d), BF),
            jax.ShapeDtypeStruct((edges, 1), F32),
            jax.ShapeDtypeStruct((nodes, d), BF),
        ),
        in_specs=[
            SMEM,
            rows(d),
            whole(ext.shape),
            line,
            line,
            whole(w1.shape),
            whole(w2.shape),
            whole(gain.shape),
        ],
        out_specs=(rows(d), rows(d), rows(d), rows(1), whole((nodes, d))),
        scratch_shapes=[pltpu.VMEM((nodes, d), F32)],
        compiler_params=pltpu.CompilerParams(
            dimension_semantics=("arbitrary",), vmem_limit_bytes=LIMIT
        ),
        name="edge_forward",
    )(count, el, ext, snd_r, rcv_r, w1, w2, gain)


def node_kernel(
    agg, lat, cot, w1, w2, gain, gagg_o, part_o, dw1_o, dw2_o, other, mine, send, recv, local
):
    p, g = lax.axis_index("patch"), lax.axis_index("grp")
    mate = (p, 1 - g)
    d = lat.shape[1]
    greet([mate])
    swap = remote(agg.at[1 - g], other, send.at[0], recv.at[0], mate)
    swap.start()
    lat_bf = lat[...].astype(BF)
    pre = dot(lat_bf, w1[0:d, :])
    swap.wait()
    agg_bf = (agg[g].astype(F32) + other[...].astype(F32)).astype(BF)
    pre += dot(agg_bf, w1[d : 2 * d, :])
    act, slope, normed, inv = mlp_tail(pre, w2[...])
    gout = norm_backward(cot[...], gain[...], normed, inv)
    gpre = (dot_nt(gout, w2[...]) * slope).astype(BF)
    mine[...] = dot_nt(gpre, w1[d : 2 * d, :]).astype(BF)
    keep = pltpu.make_async_copy(mine, gagg_o.at[g], local)
    keep.start()
    give = remote(mine, gagg_o.at[g], send.at[1], recv.at[1], mate)
    give.start()
    part_o[...] = cot[...] + dot_nt(gpre, w1[0:d, :])
    dw2_o[...] = dot_tn(act, gout).astype(BF)
    dw1_o[0:d, :] = dot_tn(lat_bf, gpre).astype(BF)
    dw1_o[d : 2 * d, :] = dot_tn(agg_bf, gpre).astype(BF)
    keep.wait()
    give.wait()


def node_layer(agg, lat, cot, w1, w2, gain):
    rows, d = lat.shape
    return pl.pallas_call(
        node_kernel,
        out_shape=(
            jax.ShapeDtypeStruct((2, rows, d), BF),
            jax.ShapeDtypeStruct((rows, d), F32),
            jax.ShapeDtypeStruct(w1.shape, BF),
            jax.ShapeDtypeStruct(w2.shape, BF),
        ),
        in_specs=[VMEM] * 6,
        out_specs=(VMEM,) * 4,
        scratch_shapes=[
            pltpu.VMEM((rows, d), BF),
            pltpu.VMEM((rows, d), BF),
            pltpu.SemaphoreType.DMA((2,)),
            pltpu.SemaphoreType.DMA((2,)),
            pltpu.SemaphoreType.DMA,
        ],
        compiler_params=comm_params(1),
        name="node_layer",
    )(agg, lat, cot, w1, w2, gain)


def backward_kernel(
    count, el, ec, act, slope, normed, inv, gagg, ext, snd_r, rcv_r, w1, w2, gain,
    grad_o, sent_o, dw1_o, dw2_o, by_s, by_r, dwe, dw2,
):
    i = pl.program_id(0)
    tile, d = el.shape
    nodes = gagg.shape[0]

    @pl.when(i == 0)
    def _():
        by_s[...] = jnp.zeros_like(by_s)
        by_r[...] = jnp.zeros_like(by_r)
        dwe[...] = jnp.zeros_like(dwe)
        dw2[...] = jnp.zeros_like(dw2)

    slot = i * tile + lax.broadcasted_iota(jnp.int32, (tile, 1), 0)
    back = dot(hot_rows(column(rcv_r[...]), nodes), gagg[...])
    gupd = jnp.where(slot < count[0], ec[...] + back, 0.0)
    gout = norm_backward(gupd, gain[...], normed[...].astype(F32), inv[...])
    gpre = (dot_nt(gout, w2[...]) * slope[...].astype(F32)).astype(BF)
    grad_o[...] = ec[...] + dot_nt(gpre, w1[0:d, :])
    dw2[...] += dot_tn(act[...], gout)
    dwe[...] += dot_tn(el[...].astype(BF), gpre)
    by_s[...] += dot(hot_cols(snd_r[...], 3 * nodes), gpre)
    by_r[...] += dot(hot_cols(rcv_r[...], nodes), gpre)

    @pl.when(i == pl.num_programs(0) - 1)
    def _():
        dw2_o[...] = dw2[...].astype(BF)
        dw1_o[0:d, :] = dwe[...].astype(BF)
        s_bf = by_s[...].astype(BF)
        r_bf = by_r[...].astype(BF)
        dw1_o[d : 2 * d, :] = dot_tn(ext[...], s_bf).astype(BF)
        dw1_o[2 * d : 3 * d, :] = dot_tn(ext[nodes : 2 * nodes, :], r_bf).astype(BF)
        spread = dot_nt(s_bf, w1[d : 2 * d, :])
        sent_o[0:nodes, :] = spread[0:nodes].astype(BF)
        kept = spread[nodes : 2 * nodes] + dot_nt(r_bf, w1[2 * d : 3 * d, :])
        sent_o[nodes : 2 * nodes, :] = kept.astype(BF)
        sent_o[2 * nodes : 3 * nodes, :] = spread[2 * nodes : 3 * nodes].astype(BF)


def edge_backward(
    count, el, ec, act, slope, normed, inv, gagg, ext, snd_r, rcv_r, w1, w2, gain, tiles
):
    edges, d = el.shape
    nodes = gagg.shape[0]
    tile = edges // tiles

    def rows(width):
        return pl.BlockSpec((tile, width), lambda i: (i, 0))

    line = pl.BlockSpec((1, tile), lambda i: (0, i))
    return pl.pallas_call(
        backward_kernel,
        grid=(tiles,),
        out_shape=(
            jax.ShapeDtypeStruct((edges, d), F32),
            jax.ShapeDtypeStruct((3 * nodes, d), BF),
            jax.ShapeDtypeStruct(w1.shape, BF),
            jax.ShapeDtypeStruct(w2.shape, BF),
        ),
        in_specs=[
            SMEM, rows(d), rows(d), rows(d), rows(d), rows(d), rows(1),
            whole(gagg.shape), whole(ext.shape), line, line,
            whole(w1.shape), whole(w2.shape), whole(gain.shape),
        ],
        out_specs=(rows(d), whole((3 * nodes, d)), whole(w1.shape), whole(w2.shape)),
        scratch_shapes=[
            pltpu.VMEM((3 * nodes, d), F32),
            pltpu.VMEM((nodes, d), F32),
            pltpu.VMEM((d, d), F32),
            pltpu.VMEM((d, d), F32),
        ],
        compiler_params=pltpu.CompilerParams(
            dimension_semantics=("arbitrary",), vmem_limit_bytes=LIMIT
        ),
        name="edge_backward",
    )(count, el, ec, act, slope, normed, inv, gagg, ext, snd_r, rcv_r, w1, w2, gain)


def plan_of(rows, sizes, order):
    steps = []
    for axis in order:
        n = sizes[axis]
        if n > 1:
            left = rows // n if rows % (16 * n) == 0 else rows
            steps.append((axis, n, rows, left))
            rows = left
    return steps


class Reducer:
    def __init__(self, n, sets, d):
        self.n, self.sets, self.d = n, sets, d
        self.sizes = axis_sizes(n)
        x, y, _ = self.sizes
        self.strides = (1, x, x * y)
        orders = ((0, 1, 2), (1, 0, 2))
        self.wide = d // 2
        self.plans = [[plan_of(size, self.sizes, o) for o in orders] for _, _, size in sets]
        self.depth = len(self.plans[0][0])
        self.slots = {}
        self.scratch = {}
        for s, (_, _, size) in enumerate(sets):
            self.scratch["in", s] = pltpu.VMEM((size, d), BF)
            self.scratch["cur", s] = pltpu.VMEM((size, d), F32)
            self.scratch["out", s] = pltpu.VMEM((size, d), BF)
            self.slots["in", s] = len(self.slots)
            for c in range(2):
                for k, (axis, m, r, left) in enumerate(self.plans[s][c]):
                    self.scratch["rx", s, c, k] = pltpu.VMEM((m - 1, left, self.wide), BF)
                    self.scratch["acc", s, c, k] = pltpu.VMEM((left, self.wide), F32)
                    self.scratch["tx", s, c, k] = pltpu.VMEM((left, self.wide), BF)
                    for step in range(1, m):
                        self.slots["sum", s, c, k, step] = len(self.slots)
                        if left < r:
                            self.slots["all", s, c, k, step] = len(self.slots)
        self.scratch["send"] = pltpu.SemaphoreType.DMA((len(self.slots),))
        self.scratch["recv"] = pltpu.SemaphoreType.DMA((len(self.slots),))

    def bind(self, parts, outs, refs):
        self.parts, self.outs = parts, outs
        self.ref = dict(zip(self.scratch, refs))
        p, g = lax.axis_index("patch"), lax.axis_index("grp")
        self.p, self.g = p, g
        nx, ny, _ = self.sizes
        self.here = (lax.rem(p, nx), lax.rem(p // nx, ny), p // (nx * ny))
        self.mate = (p, 1 - g)

    def along(self, axis, step):
        c = self.here[axis]
        t = lax.rem(c + step, self.sizes[axis])
        return t, (self.p + (t - c) * self.strides[axis], self.g)

    def peers(self):
        return [self.along(a, step)[1] for a in range(3) for step in range(1, self.sizes[a])]

    def copy(self, key, src, dst, device):
        k = self.slots[key]
        return remote(src, dst, self.ref["send"].at[k], self.ref["recv"].at[k], device)

    @staticmethod
    def window(ref, start, size, first, wide):
        if not isinstance(start, int):
            start = pl.multiple_of(start, 16)
        return ref.at[pl.ds(start, size), pl.ds(first, wide)]

    def offset(self, s, c, depth):
        at = self.sets[s][1]
        for axis, m, r, left in self.plans[s][c][:depth]:
            if left < r:
                at = at + self.here[axis] * left
        return at

    def swap(self, s):
        a, at, size = self.sets[s]
        src = self.parts[a].at[1 - self.g, pl.ds(at, size)]
        return [self.copy(("in", s), src, self.ref["in", s], self.mate)]

    def sums(self, s, k):
        made = []
        for c in range(2):
            axis, m, r, left = self.plans[s][c][k]
            base = self.ref["out", s] if k == 0 else self.ref["tx", s, c, k - 1]
            first = c * self.wide if k == 0 else 0
            for step in range(1, m):
                t, device = self.along(axis, step)
                src = self.window(base, t * left if left < r else 0, left, first, self.wide)
                dst = self.ref["rx", s, c, k].at[step - 1]
                made.append(self.copy(("sum", s, c, k, step), src, dst, device))
        return made

    def gathers(self, s, k):
        made = []
        for c in range(2):
            axis, m, r, left = self.plans[s][c][k]
            if left == r:
                continue
            out = self.outs[self.sets[s][0]]
            block = self.window(out, self.offset(s, c, k + 1), left, c * self.wide, self.wide)
            for step in range(1, m):
                made.append(self.copy(("all", s, c, k, step), block, block, self.along(axis, step)[1]))
        return made

    def begin(self, s):
        for copy in self.swap(s):
            copy.start()

    def event(self, s, k):
        depth = self.depth
        if k == 0:
            a, at, size = self.sets[s]
            for copy in self.swap(s):
                copy.wait_recv()
            total = self.parts[a][self.g, at : at + size].astype(F32) + self.ref["in", s][...].astype(F32)
            self.ref["cur", s][...] = total
            self.ref["out", s][...] = total.astype(BF)
            for copy in self.sums(s, 0):
                copy.start()
        elif k <= depth:
            k -= 1
            for copy in self.sums(s, k):
                copy.wait_recv()
            for c in range(2):
                axis, m, r, left = self.plans[s][c][k]
                mine = self.here[axis] * left if left < r else 0
                base = self.ref["cur", s] if k == 0 else self.ref["acc", s, c, k - 1]
                first = c * self.wide if k == 0 else 0
                total = self.window(base, mine, left, first, self.wide)[...]
                for step in range(m - 1):
                    total += self.ref["rx", s, c, k][step].astype(F32)
                if k < depth - 1:
                    self.ref["acc", s, c, k][...] = total
                    self.ref["tx", s, c, k][...] = total.astype(BF)
                else:
                    out = self.outs[self.sets[s][0]]
                    block = self.window(out, self.offset(s, c, depth), left, c * self.wide, self.wide)
                    block[...] = total.astype(BF)
            for copy in self.sums(s, k + 1) if k < depth - 1 else self.gathers(s, k):
                copy.start()
        else:
            k = 2 * depth - k
            for copy in self.gathers(s, k):
                copy.wait_recv()
            if k > 0:
                for copy in self.gathers(s, k - 1):
                    copy.start()

    def events(self):
        return 2 * self.depth + 1

    def drain(self):
        for s in range(len(self.sets)):
            made = self.swap(s)
            for k in range(self.depth):
                made += self.sums(s, k) + self.gathers(s, k)
            for copy in made:
                copy.wait_send()


class Homing:
    def __init__(self, n, rows, d):
        self.n = n
        self.scratch = {
            "sin": pltpu.VMEM((3, rows, d), BF),
            "home": pltpu.VMEM((2, rows, d), BF),
            "from": pltpu.VMEM((2, rows, d), BF),
            "send": pltpu.SemaphoreType.DMA((5,)),
            "recv": pltpu.SemaphoreType.DMA((5,)),
        }

    def bind(self, sent, share, refs):
        self.sent, self.share = sent, share
        self.ref = dict(zip(self.scratch, refs))
        p, self.g = lax.axis_index("patch"), lax.axis_index("grp")
        self.mate = (p, 1 - self.g)
        self.after = (lax.rem(p + 1, self.n), self.g)
        self.before = (lax.rem(p + self.n - 1, self.n), self.g)

    def peers(self):
        return [self.mate, self.after, self.before]

    def copy(self, k, src, dst, device):
        return remote(src, dst, self.ref["send"].at[k], self.ref["recv"].at[k], device)

    def swaps(self):
        return [
            self.copy(k, self.sent.at[k, 1 - self.g], self.ref["sin"].at[k], self.mate)
            for k in range(3)
        ]

    def moves(self):
        home, got = self.ref["home"], self.ref["from"]
        return [
            self.copy(3, home.at[0], got.at[0], self.before),
            self.copy(4, home.at[1], got.at[1], self.after),
        ]

    def start(self):
        for copy in self.swaps():
            copy.start()

    def turn(self):
        for copy in self.swaps():
            copy.wait_recv()
        for k in (0, 2):
            total = self.sent[k, self.g].astype(F32) + self.ref["sin"][k].astype(F32)
            self.ref["home"][k // 2] = total.astype(BF)
        for copy in self.moves():
            copy.start()
        self.share[...] = self.sent[1, self.g].astype(F32) + self.ref["sin"][1].astype(F32)

    def finish(self):
        for copy in self.moves():
            copy.wait_recv()
        self.share[...] += self.ref["from"][0].astype(F32) + self.ref["from"][1].astype(F32)

    def drain(self):
        for copy in self.swaps() + self.moves():
            copy.wait_send()


def reduce_kernel(red, hom, sent, d_n1, d_n2, d_e2, d_e1, share_o, n1_o, n2_o, e2_o, e1_o, *refs):
    cut = len(red.scratch)
    red.bind((d_n1, d_n2, d_e2, d_e1), (n1_o, n2_o, e2_o, e1_o), refs[:cut])
    hom.bind(sent, share_o, refs[cut:])
    greet(hom.peers() + red.peers())
    count = len(red.sets)
    hom.start()
    for s in range(count):
        red.begin(s)
    todo = [(SKEW * k + s, k, s) for s in range(count) for k in range(1, red.events())]
    todo += [(s - 1.5, 0, s) for s in range(count)]
    todo += [(-0.8, -1, 0), (SKEW * red.depth + 0.5, -2, 0)]
    for _, k, s in sorted(todo):
        if k == -1:
            hom.turn()
        elif k == -2:
            hom.finish()
        else:
            red.event(s, k)
    red.drain()
    hom.drain()


SKEW = 2


def reduce_all(n, sent, d_n1, d_n2, d_e2, d_e1):
    _, _, rows, d = sent.shape
    parts = (d_n1, d_n2, d_e2, d_e1)
    sets = []
    for a, part in enumerate(parts):
        at, most = 0, d_n1.shape[1]
        while at < part.shape[1]:
            size = min(most, part.shape[1] - at)
            sets.append((a, at, size))
            at += size
    red, hom = Reducer(n, sets, d), Homing(n, rows, d)
    return pl.pallas_call(
        functools.partial(reduce_kernel, red, hom),
        out_shape=[jax.ShapeDtypeStruct((rows, d), F32)]
        + [jax.ShapeDtypeStruct(part.shape[1:], BF) for part in parts],
        in_specs=[VMEM] * 5,
        out_specs=[VMEM] * 5,
        scratch_shapes=list(red.scratch.values()) + list(hom.scratch.values()),
        compiler_params=comm_params(2),
        name="reduce_all",
    )(sent, *parts)


def finish_kernel(part, share, *refs):
    half = len(refs) // 2
    refs[half][...] = part[...] + share[...]
    for src, dst in zip(refs[:half], refs[half + 1 :]):
        dst[...] = src[...].astype(F32)


def finish(part, share, sums):
    steps = 4

    def blocks(x):
        return pl.BlockSpec((x.shape[0] // steps, x.shape[1]), lambda i: (i, 0))

    return pl.pallas_call(
        finish_kernel,
        grid=(steps,),
        out_shape=[jax.ShapeDtypeStruct(x.shape, F32) for x in (part, *sums)],
        in_specs=[blocks(x) for x in (part, share, *sums)],
        out_specs=[blocks(x) for x in (part, *sums)],
        name="finish",
    )(part, share, *sums)


def local(
    node_latent,
    edge_latent,
    node_cot,
    edge_cot,
    edge_w1,
    edge_w2,
    edge_gain,
    node_w1,
    node_w2,
    node_gain,
    senders,
    receivers,
    counts,
):
    n = lax.axis_size("patch")
    rows, d = node_latent.shape
    edges = edge_latent.shape[0]
    tiles = 4
    ext = exchange(node_latent, n).reshape(6 * rows, d)
    snd_r, rcv_r = senders.reshape(1, edges), receivers.reshape(1, edges)
    e_gain, n_gain = edge_gain.reshape(1, d), node_gain.reshape(1, d)
    act, slope, normed, inv, agg = edge_forward(
        counts, edge_latent, ext, snd_r, rcv_r, edge_w1, edge_w2, e_gain, tiles
    )
    gagg, part, d_n1, d_n2 = node_layer(
        agg.reshape(2, rows, d), node_latent, node_cot, node_w1, node_w2, n_gain
    )
    edge_grad, sent, d_e1, d_e2 = edge_backward(
        counts, edge_latent, edge_cot, act, slope, normed, inv, gagg.reshape(2 * rows, d), ext,
        snd_r, rcv_r, edge_w1, edge_w2, e_gain, tiles,
    )

    def halves(x):
        return x.reshape(2, x.shape[0] // 2, d)

    share, *sums = reduce_all(
        n, sent.reshape(3, 2, rows, d), halves(d_n1), halves(d_n2), halves(d_e2), halves(d_e1)
    )
    node_grad, n1, n2, e2, e1 = finish(part, share, sums)
    return node_grad, edge_grad, e1, e2, n1, n2


def solution(mesh):
    line = P(("patch", "grp"))
    block = P(("patch", "grp"), None)
    in_specs = (block,) * 4 + (P(),) * 6 + (line,) * 3
    out_specs = (block, block) + (P("grp", None),) * 4
    return jax.shard_map(local, mesh=mesh, in_specs=in_specs, out_specs=out_specs, check_vma=False)
```

time: 125 us -> 116 us (0.928)
  other arithmetic: 9.04 us -> 0 us
  Pallas kernels: 110 us -> 115 us
  local copies, waits for them, and re-layouts: 3.42 us -> 0 us
    convert_element_type x4 -> x0, other arithmetic: 7.21 us -> none  [the longest x1 2.14 us: local(): node_sum[:cut_n].astype(F32)]
    reshape x2 -> x0, local copies, waits for them, and re-layouts: 3.41 us -> none  [local(): snd_c, rcv_c = (senders.reshape(edges, 1), receivers.reshape(edges, 1))]
    pallas_call x1 -> x2, Pallas kernels: 64 us -> 67.1 us  [the longest x1 62.8 us: reduce_all(): pl.pallas_call(functools.partial(reduce_kernel, red, hom), out_shape=[jax...]
    add x1 -> x0, other arithmetic: 1.83 us -> none  [local(): part + share]
where the time goes in v2:
time: 116 us
  Pallas kernels  115 us (99%)
  between operations  1.31 us (1%)
    pallas_call x1, Pallas kernels, reduce_all(): pl.pallas_call(functools.partial(reduce_kernel, red, hom), out_shape=[jax...  62.8 us
    pallas_call x1, Pallas kernels, exchange(): pl.pallas_call(functools.partial(exchange_kernel, n), out_shape=jax.Shape...  15.2 us
    pallas_call x1, Pallas kernels, edge_backward(): pl.pallas_call(backward_kernel, grid=(tiles,), out_shape=(jax.ShapeDtypeS...  14 us
    pallas_call x1, Pallas kernels, edge_forward(): pl.pallas_call(forward_kernel, grid=(tiles,), out_shape=(jax.ShapeDtypeSt...  11 us
    pallas_call x1, Pallas kernels, node_layer(): pl.pallas_call(node_kernel, out_shape=(jax.ShapeDtypeStruct((2, rows, d),...  7.26 us
    pallas_call x1, Pallas kernels, finish(): pl.pallas_call(finish_kernel, grid=(steps,), out_shape=[jax.ShapeDtypeStr...  4.25 us

profile of v2, /device:TPU:0, one launch (start us, length us, event | category | flops | bytes accessed | tf_op | source)
XLA Modules:
  0.0 115.8 jit_solution(13640781206703265103)
XLA Ops:
  1.3 15.2 %node_exchange.1 = bf16[3,2,160,512]{3,2,1,0:T(8,128)(2,1)} custom-call(f32[160,512]{1,0:T(8,128)} %lat.1), custom_call_target="tpu_custom_call" | custom-call | tf_op jit(solution)/shard_map/node_exchange/pallas_call | solution.py:120
  16.5 11.0 %edge_forward.1 = (bf16[1024,512]{1,0:T(8,128)(2,1)}, bf16[1024,512]{1,0:T(8,128)(2,1)}, bf16[1024,512]{1,0:T(8,128)(2,1)}, f32[1024,1]{1,0:T(8,128)}, bf16[320,512]{1,0:T(8,128)(2,1)}) custom-call(s32[1]{0:T(128)S(6)} %copy.19.count, f32[1024,512]{1,0:T(8,128)} %el.3, bf16[960,512]{1,0:T(8,128)(2,1)} %bitcast.12, s32[1,1024]{1,0:T(1,128)} %bitcast.21, ...), custom_call_target="tpu_custom_call" | custom-call | tf_op jit(solution)/shard_map/edge_forward/pallas_call | solution.py:182
  27.5 7.3 %node_layer.1 = (bf16[2,160,512]{2,1,0:T(8,128)(2,1)}, f32[160,512]{1,0:T(8,128)}, bf16[1024,512]{1,0:T(8,128)(2,1)}, bf16[512,512]{1,0:T(8,128)(2,1)}) custom-call(bf16[2,160,512]{2,1,0:T(8,128)(2,1)} %bitcast.20, f32[160,512]{1,0:T(8,128)} %lat.1, f32[160,512]{1,0:T(8,128)} %cot.1, bf16[1024,512]{1,0:T(8,128)(2,1)} %w1.4, bf16[512,512]{1,0:T(8,128)(2,1)} %w2.4, ...), custom_call_target="tpu_custom_call" | custom-call | tf_op jit(solution)/shard_map/node_layer/pallas_call | solution.py:243
  34.8 14.0 %edge_backward.1 = (f32[1024,512]{1,0:T(8,128)}, bf16[960,512]{1,0:T(8,128)(2,1)}, bf16[1536,512]{1,0:T(8,128)(2,1)}, bf16[512,512]{1,0:T(8,128)(2,1)}) custom-call(s32[1]{0:T(128)S(6)} %copy.19.count, f32[1024,512]{1,0:T(8,128)} %el.3, f32[1024,512]{1,0:T(8,128)} %ec.1, bf16[1024,512]{1,0:T(8,128)(2,1)} %get-tuple-element.31.act, ...), custom_call_target="tpu_custom_call" | custom-call | tf_op jit(solution)/shard_map/edge_backward/pallas_call | solution.py:317
  48.8 62.8 %reduce_all.1 = (f32[160,512]{1,0:T(8,128)}, bf16[512,512]{1,0:T(8,128)(2,1)}, bf16[256,512]{1,0:T(8,128)(2,1)}, bf16[256,512]{1,0:T(8,128)(2,1)}, bf16[768,512]{1,0:T(8,128)(2,1)}) custom-call(bf16[3,2,160,512]{3,2,1,0:T(8,128)(2,1)} %bitcast.16, bf16[2,512,512]{2,1,0:T(8,128)(2,1)} %bitcast.15, bf16[2,256,512]{2,1,0:T(8,128)(2,1)} %bitcast.17, ...), custom_call_target="tpu_custom_call" | custom-call | tf_op jit(solution)/shard_map/reduce_all/pallas_call | solution.py:604
  111.6 4.3 %finish.1 = (f32[160,512]{1,0:T(8,128)}, f32[512,512]{1,0:T(8,128)}, f32[256,512]{1,0:T(8,128)}, f32[256,512]{1,0:T(8,128)}, f32[768,512]{1,0:T(8,128)}) custom-call(f32[160,512]{1,0:T(8,128)} %get-tuple-element.30.part, f32[160,512]{1,0:T(8,128)} %get-tuple-element.41.share, bf16[512,512]{1,0:T(8,128)(2,1)} %get-tuple-element.42.refs_0_, ...), custom_call_target="tpu_custom_call" | custom-call | tf_op jit(solution)/shard_map/finish/pallas_call | solution.py:629

commit v3 on v2

--- a/solution.py
+++ b/solution.py
@@ -260,86 +260,6 @@
         compiler_params=comm_params(1),
         name="node_layer",
     )(agg, lat, cot, w1, w2, gain)
-
-
-def backward_kernel(
-    count, el, ec, act, slope, normed, inv, gagg, ext, snd_r, rcv_r, w1, w2, gain,
-    grad_o, sent_o, dw1_o, dw2_o, by_s, by_r, dwe, dw2,
-):
-    i = pl.program_id(0)
-    tile, d = el.shape
-    nodes = gagg.shape[0]
-
-    @pl.when(i == 0)
-    def _():
-        by_s[...] = jnp.zeros_like(by_s)
-        by_r[...] = jnp.zeros_like(by_r)
-        dwe[...] = jnp.zeros_like(dwe)
-        dw2[...] = jnp.zeros_like(dw2)
-
-    slot = i * tile + lax.broadcasted_iota(jnp.int32, (tile, 1), 0)
-    back = dot(hot_rows(column(rcv_r[...]), nodes), gagg[...])
-    gupd = jnp.where(slot < count[0], ec[...] + back, 0.0)
-    gout = norm_backward(gupd, gain[...], normed[...].astype(F32), inv[...])
-    gpre = (dot_nt(gout, w2[...]) * slope[...].astype(F32)).astype(BF)
-    grad_o[...] = ec[...] + dot_nt(gpre, w1[0:d, :])
-    dw2[...] += dot_tn(act[...], gout)
-    dwe[...] += dot_tn(el[...].astype(BF), gpre)
-    by_s[...] += dot(hot_cols(snd_r[...], 3 * nodes), gpre)
-    by_r[...] += dot(hot_cols(rcv_r[...], nodes), gpre)
-
-    @pl.when(i == pl.num_programs(0) - 1)
-    def _():
-        dw2_o[...] = dw2[...].astype(BF)
-        dw1_o[0:d, :] = dwe[...].astype(BF)
-        s_bf = by_s[...].astype(BF)
-        r_bf = by_r[...].astype(BF)
-        dw1_o[d : 2 * d, :] = dot_tn(ext[...], s_bf).astype(BF)
-        dw1_o[2 * d : 3 * d, :] = dot_tn(ext[nodes : 2 * nodes, :], r_bf).astype(BF)
-        spread = dot_nt(s_bf, w1[d : 2 * d, :])
-        sent_o[0:nodes, :] = spread[0:nodes].astype(BF)
-        kept = spread[nodes : 2 * nodes] + dot_nt(r_bf, w1[2 * d : 3 * d, :])
-        sent_o[nodes : 2 * nodes, :] = kept.astype(BF)
-        sent_o[2 * nodes : 3 * nodes, :] = spread[2 * nodes : 3 * nodes].astype(BF)
-
-
-def edge_backward(
-    count, el, ec, act, slope, normed, inv, gagg, ext, snd_r, rcv_r, w1, w2, gain, tiles
-):
-    edges, d = el.shape
-    nodes = gagg.shape[0]
-    tile = edges // tiles
-
-    def rows(width):
-        return pl.BlockSpec((tile, width), lambda i: (i, 0))
-
-    line = pl.BlockSpec((1, tile), lambda i: (0, i))
-    return pl.pallas_call(
-        backward_kernel,
-        grid=(tiles,),
-        out_shape=(
-            jax.ShapeDtypeStruct((edges, d), F32),
-            jax.ShapeDtypeStruct((3 * nodes, d), BF),
-            jax.ShapeDtypeStruct(w1.shape, BF),
-            jax.ShapeDtypeStruct(w2.shape, BF),
-        ),
-        in_specs=[
-            SMEM, rows(d), rows(d), rows(d), rows(d), rows(d), rows(1),
-            whole(gagg.shape), whole(ext.shape), line, line,
-            whole(w1.shape), whole(w2.shape), whole(gain.shape),
-        ],
-        out_specs=(rows(d), whole((3 * nodes, d)), whole(w1.shape), whole(w2.shape)),
-        scratch_shapes=[
-            pltpu.VMEM((3 * nodes, d), F32),
-            pltpu.VMEM((nodes, d), F32),
-            pltpu.VMEM((d, d), F32),
-            pltpu.VMEM((d, d), F32),
-        ],
-        compiler_params=pltpu.CompilerParams(
-            dimension_semantics=("arbitrary",), vmem_limit_bytes=LIMIT
-        ),
-        name="edge_backward",
-    )(count, el, ec, act, slope, normed, inv, gagg, ext, snd_r, rcv_r, w1, w2, gain)
 
 
 def plan_of(rows, sizes, order):
@@ -564,63 +484,160 @@
             copy.wait_send()
 
 
-def reduce_kernel(red, hom, sent, d_n1, d_n2, d_e2, d_e1, share_o, n1_o, n2_o, e2_o, e1_o, *refs):
+def backward_kernel(
+    red, hom, count, el, ec, act, slope, normed, inv, gagg, ext, snd_r, rcv_r, w1, w2, gain, d_n1, d_n2,
+    gin_o, share_o, n1_o, n2_o, e2_o, e1_o,
+    by_s, by_r, dwe, dw2, sent, d_e2, d_e1, n1_s, n2_s, e2_s, e1_s, *refs,
+):
+    i = pl.program_id(0)
+    last = pl.num_programs(0) - 1
+    tile, d = el.shape
+    nodes = gagg.shape[0]
     cut = len(red.scratch)
-    red.bind((d_n1, d_n2, d_e2, d_e1), (n1_o, n2_o, e2_o, e1_o), refs[:cut])
+    red.bind((d_n1, d_n2, d_e2, d_e1), (n1_s, n2_s, e2_s, e1_s), refs[:cut])
     hom.bind(sent, share_o, refs[cut:])
-    greet(hom.peers() + red.peers())
-    count = len(red.sets)
-    hom.start()
-    for s in range(count):
-        red.begin(s)
-    todo = [(SKEW * k + s, k, s) for s in range(count) for k in range(1, red.events())]
-    todo += [(s - 1.5, 0, s) for s in range(count)]
-    todo += [(-0.8, -1, 0), (SKEW * red.depth + 0.5, -2, 0)]
-    for _, k, s in sorted(todo):
-        if k == -1:
-            hom.turn()
-        elif k == -2:
-            hom.finish()
-        else:
-            red.event(s, k)
-    red.drain()
-    hom.drain()
+    early = [s for s in range(len(red.sets)) if red.sets[s][0] < 2]
+    late = [s for s in range(len(red.sets)) if red.sets[s][0] >= 2]
+
+    @pl.when(i == 0)
+    def _():
+        greet(hom.peers() + red.peers())
+        for s in early:
+            red.begin(s)
+        by_s[...] = jnp.zeros_like(by_s)
+        by_r[...] = jnp.zeros_like(by_r)
+        dwe[...] = jnp.zeros_like(dwe)
+        dw2[...] = jnp.zeros_like(dw2)
+
+    @pl.when(i == last - 1)
+    def _():
+        for s in early:
+            red.event(s, 0)
+
+    slot = i * tile + lax.broadcasted_iota(jnp.int32, (tile, 1), 0)
+    back = dot(hot_rows(column(rcv_r[...]), nodes), gagg[...])
+    gupd = jnp.where(slot < count[0], ec[...] + back, 0.0)
+    gout = norm_backward(gupd, gain[...], normed[...].astype(F32), inv[...])
+    dw2[...] += dot_tn(act[...], gout)
+    gpre = (dot_nt(gout, w2[...]) * slope[...].astype(F32)).astype(BF)
+    by_s[...] += dot(hot_cols(snd_r[...], 3 * nodes), gpre)
+    by_r[...] += dot(hot_cols(rcv_r[...], nodes), gpre)
+    dwe[...] += dot_tn(el[...].astype(BF), gpre)
+    gin_o[...] = dot_nt(gpre, w1[0:d, :]).astype(BF)
+
+    @pl.when(i == last)
+    def _():
+        half = d_e2.shape[1]
+        d_e2[0] = dw2[0:half, :].astype(BF)
+        d_e2[1] = dw2[half:d, :].astype(BF)
+        begun = [s for s in late if red.sets[s][0] == 2]
+        for s in begun:
+            red.begin(s)
+        red.event(early[0], 1)
+        s_bf = by_s[...].astype(BF)
+        r_bf = by_r[...].astype(BF)
+        rows = nodes // 2
+        for k in (0, 2, 1):
+            spread = dot_nt(s_bf[k * nodes : (k + 1) * nodes], w1[d : 2 * d, :])
+            if k == 1:
+                spread += dot_nt(r_bf, w1[2 * d : 3 * d, :])
+            sent[k, 0] = spread[0:rows].astype(BF)
+            sent[k, 1] = spread[rows:nodes].astype(BF)
+        hom.start()
+        d_e1[0, 0:d, :] = dwe[...].astype(BF)
+        side = dot_tn(ext[...], s_bf).astype(BF)
+        size = d_e1.shape[1]
+        d_e1[0, d:size, :] = side[0 : size - d]
+        d_e1[1, 0 : 2 * d - size, :] = side[size - d : d]
+        d_e1[1, 2 * d - size : size, :] = dot_tn(ext[nodes : 2 * nodes, :], r_bf).astype(BF)
+        for s in late:
+            if s not in begun:
+                red.begin(s)
+        todo = [(SKEW * (k - 2) + s, k, s) for s in early for k in range(1, red.events())]
+        todo += [(SKEW * k + at, k, s) for at, s in enumerate(late) for k in range(1, red.events())]
+        todo += [(at - 0.5, 0, s) for at, s in enumerate(late)]
+        todo += [(-0.4, -1, 0), (SKEW * 2 * red.depth, -2, 0)]
+        todo.remove((SKEW * -1 + early[0], 1, early[0]))
+        for _, k, s in sorted(todo):
+            if k == -1:
+                hom.turn()
+            elif k == -2:
+                hom.finish()
+            else:
+                red.event(s, k)
+        for out, kept in ((n1_o, n1_s), (n2_o, n2_s), (e2_o, e2_s), (e1_o, e1_s)):
+            out[...] = kept[...]
+        red.drain()
+        hom.drain()
 
 
 SKEW = 2
 
 
-def reduce_all(n, sent, d_n1, d_n2, d_e2, d_e1):
-    _, _, rows, d = sent.shape
-    parts = (d_n1, d_n2, d_e2, d_e1)
+def edge_backward(
+    n, count, el, ec, act, slope, normed, inv, gagg, ext, snd_r, rcv_r, w1, w2, gain, d_n1, d_n2, tiles
+):
+    edges, d = el.shape
+    nodes = gagg.shape[0]
+    tile = edges // tiles
+
+    def rows(width):
+        return pl.BlockSpec((tile, width), lambda i: (i, 0))
+
+    def cube(shape):
+        return pl.BlockSpec(shape, lambda i: (0, 0, 0), pipeline_mode=pl.Buffered(1))
+
+    line = pl.BlockSpec((1, tile), lambda i: (0, i))
+    sizes = (d_n1.shape[1], d_n2.shape[1], w2.shape[0] // 2, w1.shape[0] // 2)
     sets = []
-    for a, part in enumerate(parts):
-        at, most = 0, d_n1.shape[1]
-        while at < part.shape[1]:
-            size = min(most, part.shape[1] - at)
-            sets.append((a, at, size))
-            at += size
-    red, hom = Reducer(n, sets, d), Homing(n, rows, d)
+    for a, size in enumerate(sizes):
+        at = 0
+        while at < size:
+            sets.append((a, at, min(d, size - at)))
+            at += d
+    red, hom = Reducer(n, sets, d), Homing(n, nodes // 2, d)
     return pl.pallas_call(
-        functools.partial(reduce_kernel, red, hom),
-        out_shape=[jax.ShapeDtypeStruct((rows, d), F32)]
-        + [jax.ShapeDtypeStruct(part.shape[1:], BF) for part in parts],
-        in_specs=[VMEM] * 5,
-        out_specs=[VMEM] * 5,
-        scratch_shapes=list(red.scratch.values()) + list(hom.scratch.values()),
-        compiler_params=comm_params(2),
-        name="reduce_all",
-    )(sent, *parts)
-
-
-def finish_kernel(part, share, *refs):
-    half = len(refs) // 2
+        functools.partial(backward_kernel, red, hom),
+        grid=(tiles,),
+        out_shape=[jax.ShapeDtypeStruct((edges, d), BF), jax.ShapeDtypeStruct((nodes // 2, d), F32)]
+        + [jax.ShapeDtypeStruct((size, d), BF) for size in sizes],
+        in_specs=[
+            SMEM, rows(d), rows(d), rows(d), rows(d), rows(d), rows(1),
+            whole(gagg.shape), whole(ext.shape), line, line,
+            whole(w1.shape), whole(w2.shape), whole(gain.shape), cube(d_n1.shape), cube(d_n2.shape),
+        ],
+        out_specs=[rows(d), whole((nodes // 2, d))] + [whole((size, d)) for size in sizes],
+        scratch_shapes=[
+            pltpu.VMEM((3 * nodes, d), F32),
+            pltpu.VMEM((nodes, d), F32),
+            pltpu.VMEM((d, d), F32),
+            pltpu.VMEM((d, d), F32),
+            pltpu.VMEM((3, 2, nodes // 2, d), BF),
+            pltpu.VMEM((2, sizes[2], d), BF),
+            pltpu.VMEM((2, sizes[3], d), BF),
+        ]
+        + [pltpu.VMEM((size, d), BF) for size in sizes]
+        + list(red.scratch.values())
+        + list(hom.scratch.values()),
+        compiler_params=pltpu.CompilerParams(
+            dimension_semantics=("arbitrary",),
+            collective_id=2,
+            has_side_effects=True,
+            vmem_limit_bytes=LIMIT,
+        ),
+        name="edge_backward",
+    )(count, el, ec, act, slope, normed, inv, gagg, ext, snd_r, rcv_r, w1, w2, gain, d_n1, d_n2)
+
+
+def finish_kernel(part, share, ec, gin, *refs):
+    half = (len(refs) - 2) // 2
     refs[half][...] = part[...] + share[...]
-    for src, dst in zip(refs[:half], refs[half + 1 :]):
+    refs[half + 1][...] = ec[...] + gin[...].astype(F32)
+    for src, dst in zip(refs[:half], refs[half + 2 :]):
         dst[...] = src[...].astype(F32)
 
 
-def finish(part, share, sums):
+def finish(part, share, ec, gin, sums):
     steps = 4
 
     def blocks(x):
@@ -629,11 +646,12 @@
     return pl.pallas_call(
         finish_kernel,
         grid=(steps,),
-        out_shape=[jax.ShapeDtypeStruct(x.shape, F32) for x in (part, *sums)],
-        in_specs=[blocks(x) for x in (part, share, *sums)],
-        out_specs=[blocks(x) for x in (part, *sums)],
+        out_shape=[jax.ShapeDtypeStruct(x.shape, F32) for x in (part, ec, *sums)],
+        in_specs=[blocks(x) for x in (part, share, ec, gin, *sums)],
+        out_specs=[blocks(x) for x in (part, ec, *sums)],
+        compiler_params=pltpu.CompilerParams(vmem_limit_bytes=LIMIT),
         name="finish",
-    )(part, share, *sums)
+    )(part, share, ec, gin, *sums)
 
 
 def local(
@@ -664,18 +682,15 @@
     gagg, part, d_n1, d_n2 = node_layer(
         agg.reshape(2, rows, d), node_latent, node_cot, node_w1, node_w2, n_gain
     )
-    edge_grad, sent, d_e1, d_e2 = edge_backward(
-        counts, edge_latent, edge_cot, act, slope, normed, inv, gagg.reshape(2 * rows, d), ext,
-        snd_r, rcv_r, edge_w1, edge_w2, e_gain, tiles,
-    )
 
     def halves(x):
         return x.reshape(2, x.shape[0] // 2, d)
 
-    share, *sums = reduce_all(
-        n, sent.reshape(3, 2, rows, d), halves(d_n1), halves(d_n2), halves(d_e2), halves(d_e1)
+    gin, share, *sums = edge_backward(
+        n, counts, edge_latent, edge_cot, act, slope, normed, inv, gagg.reshape(2 * rows, d), ext,
+        snd_r, rcv_r, edge_w1, edge_w2, e_gain, halves(d_n1), halves(d_n2), tiles,
     )
-    node_grad, n1, n2, e2, e1 = finish(part, share, sums)
+    node_grad, edge_grad, n1, n2, e2, e1 = finish(part, share, edge_cot, gin, sums)
     return node_grad, edge_grad, e1, e2, n1, n2
 
 

time: 116 us -> 101 us (0.87)
  Pallas kernels: 115 us -> 99.3 us
    pallas_call x2 -> x1, Pallas kernels: 76.8 us -> 60.2 us  [edge_backward(): pl.pallas_call(functools.partial(backward_kernel, red, hom), grid=(tiles,...]
    pallas_call x1, Pallas kernels: 4.25 us -> 5.63 us  [finish(): pl.pallas_call(finish_kernel, grid=(steps,), out_shape=[jax.ShapeDtypeStr...]
where the time goes in v3:
time: 101 us
  Pallas kernels  99.3 us (98%)
  between operations  1.31 us (1%)
    pallas_call x1, Pallas kernels, edge_backward(): pl.pallas_call(functools.partial(backward_kernel, red, hom), grid=(tiles,...  60.2 us
    pallas_call x1, Pallas kernels, exchange(): pl.pallas_call(functools.partial(exchange_kernel, n), out_shape=jax.Shape...  15.2 us
    pallas_call x1, Pallas kernels, edge_forward(): pl.pallas_call(forward_kernel, grid=(tiles,), out_shape=(jax.ShapeDtypeSt...  11 us
    pallas_call x1, Pallas kernels, node_layer(): pl.pallas_call(node_kernel, out_shape=(jax.ShapeDtypeStruct((2, rows, d),...  7.18 us
    pallas_call x1, Pallas kernels, finish(): pl.pallas_call(finish_kernel, grid=(steps,), out_shape=[jax.ShapeDtypeStr...  5.63 us

profile of v3, /device:TPU:0, one launch (start us, length us, event | category | flops | bytes accessed | tf_op | source)
XLA Modules:
  0.0 100.6 jit_solution(15104181483036559883)
XLA Ops:
  1.3 15.2 %node_exchange.1 = bf16[3,2,160,512]{3,2,1,0:T(8,128)(2,1)} custom-call(f32[160,512]{1,0:T(8,128)} %lat.1), custom_call_target="tpu_custom_call" | custom-call | tf_op jit(solution)/shard_map/node_exchange/pallas_call | solution.py:120
  16.5 11.0 %edge_forward.1 = (bf16[1024,512]{1,0:T(8,128)(2,1)}, bf16[1024,512]{1,0:T(8,128)(2,1)}, bf16[1024,512]{1,0:T(8,128)(2,1)}, f32[1024,1]{1,0:T(8,128)}, bf16[320,512]{1,0:T(8,128)(2,1)}) custom-call(s32[1]{0:T(128)S(6)} %copy.19.count, f32[1024,512]{1,0:T(8,128)} %el.3, bf16[960,512]{1,0:T(8,128)(2,1)} %bitcast.9, s32[1,1024]{1,0:T(1,128)} %bitcast.15, ...), custom_call_target="tpu_custom_call" | custom-call | tf_op jit(solution)/shard_map/edge_forward/pallas_call | solution.py:182
  27.5 7.2 %node_layer.1 = (bf16[2,160,512]{2,1,0:T(8,128)(2,1)}, f32[160,512]{1,0:T(8,128)}, bf16[1024,512]{1,0:T(8,128)(2,1)}, bf16[512,512]{1,0:T(8,128)(2,1)}) custom-call(bf16[2,160,512]{2,1,0:T(8,128)(2,1)} %bitcast.14, f32[160,512]{1,0:T(8,128)} %lat.1, f32[160,512]{1,0:T(8,128)} %cot.1, bf16[1024,512]{1,0:T(8,128)(2,1)} %w1.4, bf16[512,512]{1,0:T(8,128)(2,1)} %w2.4, ...), custom_call_target="tpu_custom_call" | custom-call | tf_op jit(solution)/shard_map/node_layer/pallas_call | solution.py:243
  34.7 60.2 %edge_backward.1 = (bf16[1024,512]{1,0:T(8,128)(2,1)}, f32[160,512]{1,0:T(8,128)}, bf16[512,512]{1,0:T(8,128)(2,1)}, bf16[256,512]{1,0:T(8,128)(2,1)}, bf16[256,...) custom-call(s32[1]{0:T(128)S(6)} %copy.19.count, f32[1024,512]{1,0:T(8,128)} %el.3, f32[1024,512]{1,0:T(8,128)} %ec.3, ...), custom_call_target="tpu_custom_call" | custom-call | tf_op jit(solution)/shard_map/edge_backward/pallas_call | solution.py:599
  95.0 5.6 %finish.1 = (f32[160,512]{1,0:T(8,128)}, f32[1024,512]{1,0:T(8,128)}, f32[512,512]{1,0:T(8,128)}, f32[256,512]{1,0:T(8,128)}, f32[256,512]{1,0:T(8,128)}, /*index=5*/f32[768,512]{1,0:T(8,128)}) custom-call(f32[160,512]{1,0:T(8,128)} %get-tuple-element.28.part, f32[160,512]{1,0:T(8,128)} %get-tuple-element.36.share, f32[1024,512]{1,0:T(8,128)} %ec.3, ...), custom_call_target="tpu_custom_call" | custom-call | tf_op jit(solution)/shard_map/finish/pallas_call | solution.py:646

commit v4 on v3

--- a/solution.py
+++ b/solution.py
@@ -571,7 +571,7 @@
         hom.drain()
 
 
-SKEW = 2
+SKEW = 1
 
 
 def edge_backward(

time: 101 us -> 101 us (level)
  no operation moved by 1% of the time
where the time goes in v4:
time: 101 us
  Pallas kernels  99.5 us (99%)
  between operations  1.31 us (1%)
    pallas_call x1, Pallas kernels, edge_backward(): pl.pallas_call(functools.partial(backward_kernel, red, hom), grid=(tiles,...  60.5 us
    pallas_call x1, Pallas kernels, exchange(): pl.pallas_call(functools.partial(exchange_kernel, n), out_shape=jax.Shape...  15.2 us
    pallas_call x1, Pallas kernels, edge_forward(): pl.pallas_call(forward_kernel, grid=(tiles,), out_shape=(jax.ShapeDtypeSt...  11 us
    pallas_call x1, Pallas kernels, node_layer(): pl.pallas_call(node_kernel, out_shape=(jax.ShapeDtypeStruct((2, rows, d),...  7.18 us
    pallas_call x1, Pallas kernels, finish(): pl.pallas_call(finish_kernel, grid=(steps,), out_shape=[jax.ShapeDtypeStr...  5.63 us

profile of v4, /device:TPU:0, one launch (start us, length us, event | category | flops | bytes accessed | tf_op | source)
XLA Modules:
  0.0 100.9 jit_solution(14717534194424853977)
XLA Ops:
  1.3 15.2 %node_exchange.1 = bf16[3,2,160,512]{3,2,1,0:T(8,128)(2,1)} custom-call(f32[160,512]{1,0:T(8,128)} %lat.1), custom_call_target="tpu_custom_call" | custom-call | tf_op jit(solution)/shard_map/node_exchange/pallas_call | solution.py:120
  16.5 11.0 %edge_forward.1 = (bf16[1024,512]{1,0:T(8,128)(2,1)}, bf16[1024,512]{1,0:T(8,128)(2,1)}, bf16[1024,512]{1,0:T(8,128)(2,1)}, f32[1024,1]{1,0:T(8,128)}, bf16[320,512]{1,0:T(8,128)(2,1)}) custom-call(s32[1]{0:T(128)S(6)} %copy.19.count, f32[1024,512]{1,0:T(8,128)} %el.3, bf16[960,512]{1,0:T(8,128)(2,1)} %bitcast.9, s32[1,1024]{1,0:T(1,128)} %bitcast.15, ...), custom_call_target="tpu_custom_call" | custom-call | tf_op jit(solution)/shard_map/edge_forward/pallas_call | solution.py:182
  27.5 7.2 %node_layer.1 = (bf16[2,160,512]{2,1,0:T(8,128)(2,1)}, f32[160,512]{1,0:T(8,128)}, bf16[1024,512]{1,0:T(8,128)(2,1)}, bf16[512,512]{1,0:T(8,128)(2,1)}) custom-call(bf16[2,160,512]{2,1,0:T(8,128)(2,1)} %bitcast.14, f32[160,512]{1,0:T(8,128)} %lat.1, f32[160,512]{1,0:T(8,128)} %cot.1, bf16[1024,512]{1,0:T(8,128)(2,1)} %w1.4, bf16[512,512]{1,0:T(8,128)(2,1)} %w2.4, ...), custom_call_target="tpu_custom_call" | custom-call | tf_op jit(solution)/shard_map/node_layer/pallas_call | solution.py:243
  34.7 60.5 %edge_backward.1 = (bf16[1024,512]{1,0:T(8,128)(2,1)}, f32[160,512]{1,0:T(8,128)}, bf16[512,512]{1,0:T(8,128)(2,1)}, bf16[256,512]{1,0:T(8,128)(2,1)}, bf16[256,...) custom-call(s32[1]{0:T(128)S(6)} %copy.19.count, f32[1024,512]{1,0:T(8,128)} %el.3, f32[1024,512]{1,0:T(8,128)} %ec.3, ...), custom_call_target="tpu_custom_call" | custom-call | tf_op jit(solution)/shard_map/edge_backward/pallas_call | solution.py:599
  95.2 5.6 %finish.1 = (f32[160,512]{1,0:T(8,128)}, f32[1024,512]{1,0:T(8,128)}, f32[512,512]{1,0:T(8,128)}, f32[256,512]{1,0:T(8,128)}, f32[256,512]{1,0:T(8,128)}, /*index=5*/f32[768,512]{1,0:T(8,128)}) custom-call(f32[160,512]{1,0:T(8,128)} %get-tuple-element.28.part, f32[160,512]{1,0:T(8,128)} %get-tuple-element.36.share, f32[1024,512]{1,0:T(8,128)} %ec.3, ...), custom_call_target="tpu_custom_call" | custom-call | tf_op jit(solution)/shard_map/finish/pallas_call | solution.py:646
